TPU v7x, 32 devices: a whole 2x2x4 slice. The times are simulated.
32 devices in a mesh: rep: 2 (over y), ep: 8 (over z, core), tp: 2 (over x).
Axes of the slice: x: 2, y: 2, z: 4, core: 2. Of those that a mesh axis runs over, the one named last changes fastest.
Arguments:
- hidden_states: bfloat16 [2, 1024, 2048], P(None, ('rep', 'ep'), 'tp'), parts along dimension 1, may hold values from -8 to 8
- queries: bfloat16 [2, 1024, 4096], P(None, ('rep', 'ep'), 'tp'), parts along dimension 1, may hold values from -8 to 8
- fresh_key_value: bfloat16 [2, 1024, 2, 512], P(None, ('rep', 'ep'), None, 'tp'), parts along dimension 1, may hold values from -8 to 8
- cache: bfloat16 [16, 2, 1024, 512], P(('rep', 'ep'), None, None, 'tp'), parts along dimension 0, may hold values from -8 to 8
- cache_lengths: int32 [16], P(('rep', 'ep')), parts along dimension 0, may hold values from 1 to 1024, 4096 in all
- out_weight: bfloat16 [4096, 2048], P('tp', 'ep'), may hold values from -1 to 1
- router_weight: bfloat16 [2048, 16], P('tp'), may hold values from -0.125 to 0.125
- expert_weights: bfloat16 [16, 3, 2048, 384], P('ep', None, 'tp'), may hold values from -0.21875 to 0.21875
- expert_ids: int32 [2, 1024, 8], P(None, ('rep', 'ep')), parts along dimension 1, may hold values from 0 to 15, all different within a row; in each aligned block of 64 rows (0 to 63, 64 to 127, ..., all dimensions but the last counted through in order) at most 48 rows name the same one
- old_slots: int32 [16], replicated, may hold values from 0 to 15, as said below
- new_slots: int32 [16], replicated, may hold values from 0 to 15, as said below
- moved_experts: int32 [4], replicated, may hold values from 0 to 15, as said below
Outputs:
- mixed: bfloat16 [2, 1024, 2048], P(None, ('rep', 'ep'), 'tp'), parts along dimension 1
There are 2 independent parts, one for each index of `rep`. A program takes and returns all parts, laid end to end along the dimension named above; an argument that names none is the same for every part. Nothing has to cross between parts.
Inputs may be any that keep to these rules, and one draw needn't show every extreme that they name: `expert_ids`: each row names 8 different experts. Within the 64 rows of one request in one token block, no expert is named by more than 48 rows, a bound that some block reaches. `old_slots`: A permutation: each slot holds one expert. `new_slots`: equal to old_slots except at the moved experts, which take one another's old slots, none keeping its own. `moved_experts`: 4 different experts; no two of their old slots s share the same s // 2.
All inputs are finite; a program needn't handle non-finite values. No bound on the sum of `cache_lengths` on one device may be relied on, other than what follows from the above.
Results may differ from a plain program's by a relative error of at most 0.017.
Values may be sent and summed in bfloat16 or wider, within the bound.
A program may use at most 64 MiB of HBM per device.

v0:
```python
import jax
import jax.numpy as jnp
from jax import lax
from jax.sharding import PartitionSpec as P

D = 2048
HEAD_SIZE = 128


def lookup(entries, wanted_keys):
    return jnp.sum(
        jnp.where(
            wanted_keys[..., None] == jnp.arange(entries.shape[0], dtype=jnp.int32), entries, 0
        ),
        -1,
    )


def attend_local(queries, fresh_key_value, cache, cache_lengths):
    tokens_dev = queries.shape[1]
    kv_heads = fresh_key_value.shape[3] // HEAD_SIZE
    query_group_width = queries.shape[2] // HEAD_SIZE // kv_heads
    key_matrix = jnp.concatenate(
        [cache[0, 0], fresh_key_value[0, :, 0], fresh_key_value[1, :, 0]], 0
    )
    value_matrix = jnp.concatenate(
        [cache[0, 1], fresh_key_value[0, :, 1], fresh_key_value[1, :, 1]], 0
    )
    key_total = key_matrix.shape[0]
    context = cache.shape[2]
    query_matrix = queries.reshape(2 * tokens_dev, kv_heads, query_group_width, HEAD_SIZE)
    attention_scores = jnp.einsum(
        "meqt,wet->eqmw",
        query_matrix,
        key_matrix.reshape(key_total, kv_heads, HEAD_SIZE),
        preferred_element_type=jnp.float32,
    ) * HEAD_SIZE ** (-0.5)
    position = jnp.arange(key_total, dtype=jnp.int32)[None, :]
    row_index = jnp.arange(2 * tokens_dev, dtype=jnp.int32)[:, None]
    visible = jnp.where(
        position < context, position < cache_lengths[0], position - context <= row_index
    )
    attention_scores = jnp.where(visible, attention_scores, jnp.float32(-1e30))
    largest = jnp.max(attention_scores, -1, keepdims=True)
    weights = jnp.where(visible, jnp.exp(attention_scores - largest), jnp.float32(0.0))
    route_probability = (weights / jnp.sum(weights, -1, keepdims=True)).astype(jnp.bfloat16)
    layer_result = jnp.einsum(
        "qizo,oqx->zqix",
        route_probability,
        value_matrix.reshape(key_total, kv_heads, HEAD_SIZE),
        preferred_element_type=jnp.float32,
    )
    return layer_result.reshape(2 * tokens_dev, -1).astype(jnp.bfloat16)


def run_slots(weights, received):
    gate_up = jnp.einsum(
        "secq,egqf->secgf", received, weights[:, :2], preferred_element_type=jnp.float32
    )
    summed = lax.psum(gate_up.astype(jnp.bfloat16), "tp").astype(jnp.float32)
    hidden = (jax.nn.silu(summed[:, :, :, 0]) * summed[:, :, :, 1]).astype(jnp.bfloat16)
    layer_result = jnp.einsum(
        "secf,eqf->secq", hidden, weights[:, 2], preferred_element_type=jnp.float32
    ).astype(jnp.bfloat16)
    return lax.all_to_all(layer_result, "ep", split_axis=0, concat_axis=0, tiled=True)


def mix_block(normed_rows, resid_rows, routed, combine, slot_table, weights, capacity, groups):
    tokens_dev, top_count = routed.shape
    experts = slot_table.shape[0]
    local_slots = weights.shape[0]
    quarter = normed_rows.shape[1]
    slot_index = lookup(slot_table, routed)
    picked_mask = routed[:, :, None] == jnp.arange(experts, dtype=jnp.int32)[None, None, :]
    expert_marks = picked_mask.any(1).astype(jnp.bfloat16)
    earlier = (jnp.arange(tokens_dev)[:, None] > jnp.arange(tokens_dev)[None, :]).astype(
        jnp.bfloat16
    )
    before = jnp.dot(earlier, expert_marks, preferred_element_type=jnp.float32)
    slot_rank = jnp.sum(jnp.where(picked_mask, before[:, None, :], 0.0), -1).astype(jnp.int32)
    buffer_row = (slot_index * capacity + slot_rank).reshape(-1)
    buffer_rows = (
        jnp.zeros((groups * local_slots * capacity, quarter), jnp.bfloat16)
        .at[buffer_row]
        .set(jnp.repeat(normed_rows, top_count, axis=0))
    )
    outgoing = buffer_rows.reshape(groups, local_slots, capacity, quarter)
    returned = run_slots(
        weights, lax.all_to_all(outgoing, "ep", split_axis=0, concat_axis=0, tiled=True)
    )
    gathered = returned.reshape(-1, quarter)[buffer_row].reshape(tokens_dev, top_count, quarter)
    mixed_rows = resid_rows.astype(jnp.float32) + jnp.sum(
        combine[:, :, None] * gathered.astype(jnp.float32), 1
    )
    return mixed_rows.astype(jnp.bfloat16)


def relocate(expert_weights, old_slots, new_slots, moved_experts):
    local_slots = expert_weights.shape[0]
    groups = lax.axis_size("ep")
    flat_weights = expert_weights.reshape(local_slots, groups, -1)
    old_moved = lookup(old_slots, moved_experts)
    new_moved = lookup(new_slots, moved_experts)
    own_slots = lax.axis_index("ep") * local_slots + jnp.arange(local_slots, dtype=jnp.int32)
    leaving = (own_slots[:, None] == old_moved[None, :]).any(1)
    outgoing = jnp.sum(jnp.where(leaving[:, None, None], flat_weights, jnp.bfloat16(0.0)), 0)
    spread = lax.all_to_all(outgoing, "ep", split_axis=0, concat_axis=0, tiled=True)
    target_dev = new_moved // local_slots
    anchor_dev = old_moved // local_slots
    matches = jnp.arange(groups, dtype=jnp.int32)[:, None] == target_dev[None, :]
    anchor = jnp.sum(jnp.where(matches, anchor_dev[None, :], 0), 1)
    picked = jnp.where(matches.any(1)[:, None], spread[anchor], jnp.bfloat16(0.0))
    landed = lax.all_to_all(picked, "ep", split_axis=0, concat_axis=0, tiled=True)
    arriving = (own_slots[:, None] == new_moved[None, :]).any(1)
    return jnp.where(
        arriving[:, None, None, None],
        landed.reshape(expert_weights.shape[1:])[None],
        expert_weights,
    )


def per_device(
    hidden_states,
    queries,
    fresh_key_value,
    cache,
    cache_lengths,
    out_weight,
    router_weight,
    expert_weights,
    expert_ids,
    old_slots,
    new_slots,
    moved_experts,
):
    tokens_dev = hidden_states.shape[1]
    quarter = hidden_states.shape[2]
    experts = router_weight.shape[1]
    top_count = expert_ids.shape[2]
    groups = lax.axis_size("ep")
    capacity = min(tokens_dev, 3 * tokens_dev * top_count // (2 * experts))
    attention = attend_local(queries, fresh_key_value, cache, cache_lengths)
    head_terms = jnp.dot(
        attention,
        lax.all_gather(out_weight, "ep", axis=1, tiled=True),
        preferred_element_type=jnp.float32,
    )
    attn_out = lax.psum_scatter(
        head_terms.astype(jnp.bfloat16), "tp", scatter_dimension=1, tiled=True
    ).astype(jnp.float32)
    residual = (
        hidden_states.reshape(2 * tokens_dev, quarter).astype(jnp.float32) + attn_out
    ).astype(jnp.bfloat16)
    wide = residual.astype(jnp.float32)
    squares = lax.psum(jnp.sum(wide * wide, 1), "tp")
    normed = (wide * lax.rsqrt(squares / D + 1e-06)[:, None]).astype(jnp.bfloat16)
    logits = lax.psum(
        jnp.dot(normed, router_weight, preferred_element_type=jnp.float32).astype(jnp.bfloat16),
        "tp",
    ).astype(jnp.float32)
    routed = expert_ids.reshape(2 * tokens_dev, top_count)
    selected = jnp.sum(
        jnp.where(
            routed[:, :, None] == jnp.arange(experts, dtype=jnp.int32)[None, None, :],
            logits[:, None, :],
            0.0,
        ),
        -1,
    )
    raised = jnp.exp(selected)
    combine = raised / jnp.sum(raised, 1, keepdims=True)
    weights_two = relocate(expert_weights, old_slots, new_slots, moved_experts)
    outputs = []
    for block_index, slot_table, weights in (
        (0, old_slots, expert_weights),
        (1, new_slots, weights_two),
    ):
        lower = block_index * tokens_dev
        upper = lower + tokens_dev
        outputs.append(
            mix_block(
                normed[lower:upper],
                residual[lower:upper],
                routed[lower:upper],
                combine[lower:upper],
                slot_table,
                weights,
                capacity,
                groups,
            )
        )
    return jnp.stack(outputs)


def solution(mesh):
    return jax.shard_map(
        per_device,
        mesh=mesh,
        in_specs=(
            P(None, ("rep", "ep"), "tp"),
            P(None, ("rep", "ep"), "tp"),
            P(None, ("rep", "ep"), None, "tp"),
            P(("rep", "ep"), None, None, "tp"),
            P(("rep", "ep")),
            P("tp", "ep"),
            P("tp", None),
            P("ep", None, "tp", None),
            P(None, ("rep", "ep"), None),
            P(),
            P(),
            P(),
        ),
        out_specs=P(None, ("rep", "ep"), "tp"),
        check_vma=False,
    )
```

profile of v0, /device:TPU:0, one launch (start us, length us, event | category | flops | bytes accessed | tf_op | source)
XLA Modules:
  0.0 493.2 jit_solution(13353196676988205239)
XLA Ops:
  6.5 0.9 select_reduce_fusion.7
  7.6 4.8 select_reduce_fusion
  12.4 3.9 all_to_all.32
  16.4 0.6 broadcast.258
  17.0 15.5 %reduce.7 = bf16[8,147456]{1,0:T(8,128)(2,1)S(1)} reduce(bf16[8,1,147456]{2,1,0:T(2,128)(2,1)} %all_to_all.32, bf16[]{:T(256)} %broadcast.258), dimensions={1}, to_apply=%all_to_all.32.reduce_sub_computation | reduce | bytes 4718594 | tf_op jit(solution)/shard_map/all_to_all | solution.py:107
  32.4 3.5 reshape.319
  36.0 6.4 %all-to-all-start.2 = ((bf16[8,2,73728]{2,1,0:T(2,128)(2,1)}), bf16[8,2,73728]{2,1,0:T(2,128)(2,1)S(1)}, u32[]{:S(2)}, u32[]{:S(2)}) async-start(bf16[8,2,73728]{2,1,0:T(2,128)(2,1)} %reshape.319), calls=%async_computation.3 | async-start | bytes 4718592 | tf_op jit(solution)/shard_map/all_to_all | solution.py:107
  42.3 0.7 all-gather.2.cloned.1.call-update
  43.7 2.1 fusion.90
  45.7 1.2 copy.133
  47.0 1.0 copy.102
  48.0 1.1 copy.138
  49.4 1.8 fusion.92
  51.2 0.6 copy_bitcast_fusion.1
  51.8 1.7 fusion.61
  53.5 9.2 %fusion.94 = (f32[2,8,128]{2,1,0:T(8,128)}, f32[2,8,128,1152]{2,3,1,0:T(8,128)}) fusion(pred[128,1152]{0,1:T(8,128)(4,1)} %fusion.61, bf16[128,2,8,128]{3,2,1,0:T(8,128)(2,1)S(1)} %bitcast.180, bf16[64,2,128]{2,0,1:T(8,128)(2,1)S(1)} %get-tuple-element.35, bf16[64,2,128]{2,0,1:T(8,128)(2,1)} %get-tuple-element.36, bf16[1024,2,128]{2,0,1:T(8,128)(2,1)} %copy.102), kind=kOutput, calls=%fused_computation.146 | convolution fusion | flops 617546880 | bytes 10706944 | tf_op jit(solution)/shard_map/sub | solution.py:45
  62.8 86.9 %all-to-all-done.2 = bf16[8,2,73728]{2,1,0:T(2,128)(2,1)S(1)} async-done(((bf16[8,2,73728]{2,1,0:T(2,128)(2,1)}), bf16[8,2,73728]{2,1,0:T(2,128)(2,1)S(1)}, u32[]{:S(2)}, u32[]{:S(2)}) %all-to-all-start.2) | async-done | bytes 2359328 | tf_op jit(solution)/shard_map/all_to_all | solution.py:107
  149.6 4.6 reshape.320
  154.2 5.4 %copy.171 = bf16[8,1,147456]{2,0,1:T(8,128)(2,1)S(1)} copy(bf16[8,1,147456]{2,1,0:T(2,128)(2,1)} %reshape.320) | data formatting | bytes 4718592
  159.8 2.3 gather_fusion.2
  162.1 2.4 gather_fusion.3
  164.5 3.0 fusion.11
  167.5 3.2 reduce.8
  170.7 5.2 %reshape.321 = bf16[8,2,73728]{2,1,0:T(2,128)(2,1)} reshape(bf16[8,147456]{1,0:T(8,128)(2,1)} %reduce.8) | data formatting | bytes 4718592
  175.9 6.2 %all-to-all-start.3 = ((bf16[8,2,73728]{2,1,0:T(2,128)(2,1)}), bf16[8,2,73728]{2,1,0:T(2,128)(2,1)S(1)}, u32[]{:S(2)}, u32[]{:S(2)}) async-start(bf16[8,2,73728]{2,1,0:T(2,128)(2,1)} %reshape.321), calls=%async_computation.4 | async-start | bytes 4718592 | tf_op jit(solution)/shard_map/all_to_all | solution.py:113
  182.1 0.3 reduce-scatter.2.cloned.1.call-start
  182.4 0.7 copy.99
  183.1 0.7 copy.100
  184.1 1.0 concatenate.23
  185.1 4.6 fusion.45
  189.8 5.5 %convolution_convert_fusion = bf16[128,2048]{1,0:T(8,128)(2,1)} fusion(bf16[128,2048]{0,1:T(8,128)(2,1)S(1)} %bitcast.178, bf16[2048,2048]{1,0:T(8,128)(2,1)} %all-gather.2.cloned.1.call-done), kind=kOutput, calls=%fused_computation.23 | convolution fusion | flops 1074003968 | bytes 9437184 | tf_op jit(solution)/shard_map/dot_general | solution.py:143
  196.0 15.5 %reduce-scatter.2.cloned.1.call-done = bf16[128,1024]{1,0:T(8,128)(2,1)} async-done(((bf16[128,2048]{1,0:T(8,128)(2,1)}), bf16[128,1024]{1,0:T(8,128)(2,1)}) %reduce-scatter.2.cloned.1.call-update) | async-done | bytes 262160 | tf_op jit(solution)/shard_map/reduce_scatter | solution.py:148
  211.5 1.1 fusion.62
  212.6 4.9 %psum.28 = f32[128]{0:T(128)S(1)} all-reduce(f32[128]{0:T(128)S(1)} %get-tuple-element.13), channel_id=1, replica_groups=mesh['rep'=2,'ep'=8,'tp'=2] {'tp'}, use_global_device_ids=true, to_apply=%region_4.5 | all-reduce | flops 128 | bytes 1024 | tf_op jit(solution)/shard_map/psum | solution.py:155
  217.7 3.9 scatter_custom_fusion
  221.6 15.1 %all-to-all-done.3 = bf16[8,2,73728]{2,1,0:T(2,128)(2,1)S(1)} async-done(((bf16[8,2,73728]{2,1,0:T(2,128)(2,1)}), bf16[8,2,73728]{2,1,0:T(2,128)(2,1)S(1)}, u32[]{:S(2)}, u32[]{:S(2)}) %all-to-all-start.3) | async-done | bytes 2359328 | tf_op jit(solution)/shard_map/all_to_all | solution.py:113
  236.7 4.3 all-to-all-start
  241.3 3.8 scatter_custom_fusion.1
  245.1 33.8 %all-to-all-done = bf16[8,2,48,1024]{3,2,1,0:T(8,128)(2,1)} async-done(((bf16[8,2,48,1024]{3,2,1,0:T(8,128)(2,1)}), bf16[8,2,48,1024]{3,2,1,0:T(8,128)(2,1)}, u32[]{:S(2)}, u32[]{:S(2)}) %all-to-all-start) | async-done | bytes 1572896 | tf_op jit(solution)/shard_map/all_to_all | solution.py:89
  278.9 4.3 all-to-all-start.4
  283.2 0.3 all-reduce.3.cloned.1.call-start
  283.5 4.6 reshape.322
  288.1 14.8 %reduce.4 = bf16[8,147456]{1,0:T(8,128)(2,1)S(1)} reduce(bf16[8,1,147456]{2,1,0:T(2,128)(2,1)} %reshape.322, bf16[]{:T(256)} %constant.67), dimensions={1}, to_apply=%all_to_all.29.reduce_sub_computation | reduce | bytes 4718594 | tf_op jit(solution)/shard_map/all_to_all | solution.py:113
  302.9 2.5 broadcast_in_dim.207
  305.4 6.0 %broadcast_select_fusion = bf16[2,3,1024,384]{3,2,1,0:T(8,128)(2,1)} fusion(bf16[2,3,1024,384]{3,2,1,0:T(8,128)(2,1)} %param.19, pred[2]{0:T(512)(128)(4,1)S(1)} %get-tuple-element.8, bf16[3,1024,384]{2,1,0:T(8,128)(2,1)} %broadcast_in_dim.207), kind=kLoop, calls=%fused_computation.14 | loop fusion | flops 2359296 | bytes 11796482 | tf_op jit(solution)/shard_map/jit(_where)/select_n | solution.py:115
  311.4 3.8 fusion.33
  315.2 5.7 %all-to-all-done.4 = bf16[8,2,48,1024]{3,2,1,0:T(8,128)(2,1)} async-done(((bf16[8,2,48,1024]{3,2,1,0:T(8,128)(2,1)}), bf16[8,2,48,1024]{3,2,1,0:T(8,128)(2,1)}, u32[]{:S(2)}, u32[]{:S(2)}) %all-to-all-start.4) | async-done | bytes 1572896 | tf_op jit(solution)/shard_map/all_to_all | solution.py:89
  321.0 4.8 fusion.38
  325.7 67.7 %all-reduce.3.cloned.1.call-done = (bf16[8,2,48,2,384]{4,2,0,1,3:T(8,128)(2,1)}, bf16[8,2,48,2,384]{4,2,3,0,1:T(8,128)(2,1)}) async-done(((bf16[8,2,48,2,384]{4,2,0,1,3:T(8,128)(2,1)}, bf16[8,2,48,2,384]{4,2,3,0,1:T(8,128)(2,1)}), (bf16[8,2,48,2,384]{4,2,0,1,3:T(8,128)(2,1)}, bf16[8,2,48,2,384]{4,2,3,0,1:T(8,128)(2,1)})) %all-reduce.3.cloned.1.call-update) | async-done | bytes 2359312 | tf_op jit(solution)/shard_map/psum | solution.py:60
  393.5 1.5 convert_element_type.157
  394.9 2.5 fusion.32
  397.4 1.3 copy.120
  398.7 4.7 all-to-all-start.5
  403.7 2.5 fusion.29
  406.2 1.3 copy.113
  407.5 33.7 %all-to-all-done.5 = bf16[8,2,48,1024]{3,2,1,0:T(8,128)(2,1)S(1)} async-done(((bf16[8,2,48,1024]{3,2,1,0:T(8,128)(2,1)}), bf16[8,2,48,1024]{3,2,1,0:T(8,128)(2,1)S(1)}, u32[]{:S(2)}, u32[]{:S(2)}) %all-to-all-start.5) | async-done | bytes 1572896 | tf_op jit(solution)/shard_map/all_to_all | solution.py:65
  441.2 3.6 all-to-all-start.1
  445.1 5.2 %psum.29 = bf16[128,16]{0,1:T(8,128)(2,1)S(1)} all-reduce(bf16[128,16]{0,1:T(8,128)(2,1)S(1)} %convolution_convert_fusion.3), channel_id=1, replica_groups=mesh['rep'=2,'ep'=8,'tp'=2] {'tp'}, use_global_device_ids=true, to_apply=%region_5.6 | all-reduce | flops 2048 | bytes 8192 | tf_op jit(solution)/shard_map/psum | solution.py:157
  450.6 2.8 gather_fusion.1
  453.4 1.9 fusion.12
  455.3 27.2 %all-to-all-done.1 = bf16[8,2,48,1024]{3,2,1,0:T(8,128)(2,1)S(1)} async-done(((bf16[8,2,48,1024]{3,2,1,0:T(8,128)(2,1)}), bf16[8,2,48,1024]{3,2,1,0:T(8,128)(2,1)S(1)}, u32[]{:S(2)}, u32[]{:S(2)}) %all-to-all-start.1) | async-done | bytes 1572896 | tf_op jit(solution)/shard_map/all_to_all | solution.py:65
  482.6 2.0 gather_fusion
  484.6 0.7 fusion.13
  485.4 0.7 pad_maximum_fusion
  (72 shorter events, 2.8 us)
Async XLA Ops:
  6.5 438.4 %copy-start = (bf16[1024,16]{0,1:T(8,128)(2,1)S(1)}, bf16[1024,16]{0,1:T(8,128)(2,1)}, u32[]{:S(2)}) copy-start(bf16[1024,16]{0,1:T(8,128)(2,1)} %param.18) | copy-start | bytes 98308
  36.0 113.7 %all-to-all-start.2 = ((bf16[8,2,73728]{2,1,0:T(2,128)(2,1)}), bf16[8,2,73728]{2,1,0:T(2,128)(2,1)S(1)}, u32[]{:S(2)}, u32[]{:S(2)}) async-start(bf16[8,2,73728]{2,1,0:T(2,128)(2,1)} %reshape.319), calls=%async_computation.3 | async-start | bytes 4718592 | tf_op jit(solution)/shard_map/all_to_all | solution.py:107
  42.3 147.4 %all-gather.2.cloned.1.call-start = ((), (), s32[]{:S(2)}) async-start(), calls=%async_computation.7 | async-start | bytes 9437184 | tf_op jit(solution)/shard_map/all_gather | solution.py:145
  175.9 6.5 %copy-start.6 = (s32[2,64,8]{1,2,0:T(8,128)S(1)}, s32[2,64,8]{1,2,0:T(8,128)}, u32[]{:S(2)}) copy-start(s32[2,64,8]{1,2,0:T(8,128)} %param.20) | copy-start | bytes 12292
  175.9 6.5 %copy-start.4 = (bf16[1,64,1,256]{3,2,1,0:T(2,128)(2,1)S(1)}, bf16[1,64,1,256]{3,2,1,0:T(2,128)(2,1)}, u32[]{:S(2)}) copy-start(bf16[1,64,1,256]{3,2,1,0:T(2,128)(2,1)} %get-tuple-element.24) | copy-start | bytes 98308
  175.9 60.9 %all-to-all-start.3 = ((bf16[8,2,73728]{2,1,0:T(2,128)(2,1)}), bf16[8,2,73728]{2,1,0:T(2,128)(2,1)S(1)}, u32[]{:S(2)}, u32[]{:S(2)}) async-start(bf16[8,2,73728]{2,1,0:T(2,128)(2,1)} %reshape.321), calls=%async_computation.4 | async-start | bytes 4718592 | tf_op jit(solution)/shard_map/all_to_all | solution.py:113
  182.1 3.0 copy-start.9
  182.1 29.4 %reduce-scatter.2.cloned.1.call-start = ((), (), s32[]{:S(2)}) async-start(), calls=%async_computation.8 | async-start | bytes 786432 | tf_op jit(solution)/shard_map/reduce_scatter | solution.py:148
  189.7 5.9 %copy-start.7 = (s32[16]{0:T(128)S(1)}, s32[16]{0:T(128)}, u32[]{:S(2)}) copy-start(s32[16]{0:T(128)} %param.22) | copy-start | bytes 196
  189.8 5.9 %copy-start.8 = (s32[16]{0:T(128)S(1)}, s32[16]{0:T(128)}, u32[]{:S(2)}) copy-start(s32[16]{0:T(128)} %param.21) | copy-start | bytes 196
  189.8 21.7 %copy-start.5 = (bf16[2,64,1024]{2,1,0:T(8,128)(2,1)S(1)}, bf16[2,64,1024]{2,1,0:T(8,128)(2,1)}, u32[]{:S(2)}) copy-start(bf16[2,64,1024]{2,1,0:T(8,128)(2,1)} %param.12) | copy-start | bytes 786436
  212.6 24.1 %copy-start.1 = (bf16[128,1024]{1,0:T(8,128)(2,1)}, bf16[128,1024]{1,0:T(8,128)(2,1)S(1)}, u32[]{:S(2)}) copy-start(bf16[128,1024]{1,0:T(8,128)(2,1)S(1)} %get-tuple-element.14) | copy-start | bytes 786436
  236.7 42.1 %all-to-all-start = ((bf16[8,2,48,1024]{3,2,1,0:T(8,128)(2,1)}), bf16[8,2,48,1024]{3,2,1,0:T(8,128)(2,1)}, u32[]{:S(2)}, u32[]{:S(2)}) async-start(bf16[8,2,48,1024]{3,2,1,0:T(8,128)(2,1)} %bitcast.175), calls=%async_computation.1 | async-start | bytes 3145728 | tf_op jit(solution)/shard_map/all_to_all | solution.py:89
  278.9 42.1 %all-to-all-start.4 = ((bf16[8,2,48,1024]{3,2,1,0:T(8,128)(2,1)}), bf16[8,2,48,1024]{3,2,1,0:T(8,128)(2,1)}, u32[]{:S(2)}, u32[]{:S(2)}) async-start(bf16[8,2,48,1024]{3,2,1,0:T(8,128)(2,1)} %bitcast.174), calls=%async_computation.5 | async-start | bytes 3145728 | tf_op jit(solution)/shard_map/all_to_all | solution.py:89
  283.2 110.3 %all-reduce.3.cloned.1.call-start = ((), (), s32[]{:S(2)}) async-start(), calls=%async_computation.9 | async-start | bytes 4718592 | tf_op jit(solution)/shard_map/psum | solution.py:60
  302.9 8.5 %slice-start = ((s8[4718592]{0:T(1024)(128)(4,1)}), s8[524288]{0:T(1024)(128)(4,1)S(1)}, s32[]{:S(2)}) async-start(s8[4718592]{0:T(1024)(128)(4,1)} %bitcast.171), calls=%async_computation.10 | async-start | bytes 1048576
  305.4 6.0 %slice-start.1 = ((s8[4718592]{0:T(1024)(128)(4,1)}), s8[4194304]{0:T(1024)(128)(4,1)S(1)}, s32[]{:S(2)}) async-start(s8[4718592]{0:T(1024)(128)(4,1)} %bitcast.171), calls=%async_computation.11 | async-start | bytes 8388608
  398.7 4.7 copy-start.3
  398.7 42.5 %all-to-all-start.5 = ((bf16[8,2,48,1024]{3,2,1,0:T(8,128)(2,1)}), bf16[8,2,48,1024]{3,2,1,0:T(8,128)(2,1)S(1)}, u32[]{:S(2)}, u32[]{:S(2)}) async-start(bf16[8,2,48,1024]{3,2,1,0:T(8,128)(2,1)} %copy.120), calls=%async_computation.6 | async-start | bytes 3145728 | tf_op jit(solution)/shard_map/all_to_all | solution.py:65
  441.2 41.3 %all-to-all-start.1 = ((bf16[8,2,48,1024]{3,2,1,0:T(8,128)(2,1)}), bf16[8,2,48,1024]{3,2,1,0:T(8,128)(2,1)S(1)}, u32[]{:S(2)}, u32[]{:S(2)}) async-start(bf16[8,2,48,1024]{3,2,1,0:T(8,128)(2,1)} %copy.113), calls=%async_computation.2 | async-start | bytes 3145728 | tf_op jit(solution)/shard_map/all_to_all | solution.py:65
  482.6 2.8 copy-start.2
Sparse Core Ops, SparseCore 0:
  44.7 121.8 all-gather.1
  195.4 16.0 reduce-scatter.1
  325.9 67.5 all-reduce.2
where the time goes:
time: 500 us; the launch traced here: 493 us
  waiting for transfers between devices  286 us (57%)
  local copies, waits for them, and re-layouts  61.7 us (12%)
  other arithmetic  56.9 us (11%)
  matrix products  33.2 us (7%)
  starting transfers between devices  30.1 us (6%)
  between operations  14.7 us (3%)
  blocking collectives  10.1 us (2%)
    all_to_all x1, waiting for transfers between devices, relocate(): lax.all_to_all(outgoing, 'ep', split_axis=0, concat_axis=0, tiled=True)  86.9 us
    psum x1, waiting for transfers between devices, run_slots(): summed = lax.psum(gate_up.astype(jnp.bfloat16), 'tp').astype(jnp.float32)  67.7 us
    all_to_all x2, waiting for transfers between devices, run_slots(): lax.all_to_all(layer_result, 'ep', split_axis=0, concat_axis=0, tiled=True)  60.9 us
    all_to_all x2, waiting for transfers between devices, mix_block(): lax.all_to_all(outgoing, 'ep', split_axis=0, concat_axis=0, tiled=True)  39.5 us
    unnamed x32, local copies, waits for them, and re-layouts  25.7 us
    reduce_scatter x1, waiting for transfers between devices, per_device(): lax.psum_scatter(head_terms.astype(jnp.bfloat16), 'tp', scatter_dimension...  15.5 us
    all_to_all x1, other arithmetic, relocate(): lax.all_to_all(outgoing, 'ep', split_axis=0, concat_axis=0, tiled=True)  15.5 us
    all_to_all x1, waiting for transfers between devices, relocate(): lax.all_to_all(picked, 'ep', split_axis=0, concat_axis=0, tiled=True)  15.1 us
  transfers between devices with their start and end apart: 9, of which 8 were waited for; matrix products, arithmetic and copies ran while one was open for 22% of the time, Pallas kernels for 0%

commit v1 on v0

--- a/solution.py
+++ b/solution.py
@@ -95,28 +95,40 @@
     return mixed_rows.astype(jnp.bfloat16)
 
 
-def relocate(expert_weights, old_slots, new_slots, moved_experts):
-    local_slots = expert_weights.shape[0]
+def gathered_experts(normed, resid, routed, combine, slot_table, weights):
+    tokens_dev, quarter = normed.shape
+    experts = slot_table.shape[0]
+    local_slots = weights.shape[0]
     groups = lax.axis_size("ep")
-    flat_weights = expert_weights.reshape(local_slots, groups, -1)
-    old_moved = lookup(old_slots, moved_experts)
-    new_moved = lookup(new_slots, moved_experts)
-    own_slots = lax.axis_index("ep") * local_slots + jnp.arange(local_slots, dtype=jnp.int32)
-    leaving = (own_slots[:, None] == old_moved[None, :]).any(1)
-    outgoing = jnp.sum(jnp.where(leaving[:, None, None], flat_weights, jnp.bfloat16(0.0)), 0)
-    spread = lax.all_to_all(outgoing, "ep", split_axis=0, concat_axis=0, tiled=True)
-    target_dev = new_moved // local_slots
-    anchor_dev = old_moved // local_slots
-    matches = jnp.arange(groups, dtype=jnp.int32)[:, None] == target_dev[None, :]
-    anchor = jnp.sum(jnp.where(matches, anchor_dev[None, :], 0), 1)
-    picked = jnp.where(matches.any(1)[:, None], spread[anchor], jnp.bfloat16(0.0))
-    landed = lax.all_to_all(picked, "ep", split_axis=0, concat_axis=0, tiled=True)
-    arriving = (own_slots[:, None] == new_moved[None, :]).any(1)
-    return jnp.where(
-        arriving[:, None, None, None],
-        landed.reshape(expert_weights.shape[1:])[None],
-        expert_weights,
-    )
+    slot_index = lookup(slot_table, routed)
+    slots = jnp.arange(experts, dtype=jnp.int32)
+    by_slot = jnp.sum(
+        jnp.where(slot_index[:, :, None] == slots, combine[:, :, None], 0.0), 1
+    )
+    rows = lax.all_gather(normed, "ep", axis=0, tiled=True)
+    shares = lax.all_to_all(
+        by_slot.reshape(tokens_dev, groups, local_slots).transpose(1, 0, 2),
+        "ep",
+        split_axis=0,
+        concat_axis=0,
+        tiled=True,
+    ).reshape(groups * tokens_dev, local_slots)
+    gate_up = jnp.einsum(
+        "rq,egqf->regf", rows, weights[:, :2], preferred_element_type=jnp.float32
+    ).astype(jnp.bfloat16)
+    half = lax.psum_scatter(gate_up, "tp", scatter_dimension=0, tiled=True).astype(jnp.float32)
+    hidden = (jax.nn.silu(half[:, :, 0]) * half[:, :, 1]).astype(jnp.bfloat16)
+    hidden = lax.all_gather(hidden, "tp", axis=0, tiled=True)
+    total = 0.0
+    for slot in range(local_slots):
+        out = jnp.dot(
+            hidden[:, slot], weights[slot, 2].T, preferred_element_type=jnp.float32
+        ).astype(jnp.bfloat16)
+        total = total + shares[:, slot, None] * out.astype(jnp.float32)
+    mixed = lax.psum_scatter(
+        total.astype(jnp.bfloat16), "ep", scatter_dimension=0, tiled=True
+    ).astype(jnp.float32)
+    return (resid.astype(jnp.float32) + mixed).astype(jnp.bfloat16)
 
 
 def per_device(
@@ -138,6 +150,7 @@
     experts = router_weight.shape[1]
     top_count = expert_ids.shape[2]
     groups = lax.axis_size("ep")
+    local_slots = expert_weights.shape[0]
     capacity = min(tokens_dev, 3 * tokens_dev * top_count // (2 * experts))
     attention = attend_local(queries, fresh_key_value, cache, cache_lengths)
     head_terms = jnp.dot(
@@ -169,13 +182,11 @@
     )
     raised = jnp.exp(selected)
     combine = raised / jnp.sum(raised, 1, keepdims=True)
-    weights_two = relocate(expert_weights, old_slots, new_slots, moved_experts)
+    if groups * tokens_dev <= groups * local_slots * capacity:
+        mixed = gathered_experts(normed, residual, routed, combine, old_slots, expert_weights)
+        return mixed.reshape(2, tokens_dev, quarter)
     outputs = []
-    for block_index, slot_table, weights in (
-        (0, old_slots, expert_weights),
-        (1, new_slots, weights_two),
-    ):
-        lower = block_index * tokens_dev
+    for lower in (0, tokens_dev):
         upper = lower + tokens_dev
         outputs.append(
             mix_block(
@@ -183,8 +194,8 @@
                 residual[lower:upper],
                 routed[lower:upper],
                 combine[lower:upper],
-                slot_table,
-                weights,
+                old_slots,
+                expert_weights,
                 capacity,
                 groups,
             )

time: 500 us -> 283 us (0.57); the launches traced: 493 us -> 282 us
  waiting for transfers between devices: 286 us -> 204 us
  local copies, waits for them, and re-layouts: 61.7 us -> 3.12 us
  other arithmetic: 56.9 us -> 8.83 us
  starting transfers between devices: 30.1 us -> 0.21 us
  blocking collectives: 10.1 us -> 19.9 us
    all_to_all x6 -> x0, waiting for transfers between devices: 202 us -> none  [the longest x1 86.9 us: relocate(): lax.all_to_all(outgoing, 'ep', split_axis=0, concat_axis=0, tiled=True)]
    reduce_scatter x0 -> x2, waiting for transfers between devices: none -> 79.1 us  [the longest x1 42.9 us: gathered_experts(): lax.psum_scatter(gate_up, 'tp', scatter_dimension=0, tiled=True)]
    all_gather x1, waiting for transfers between devices: 0.02 us -> 70.5 us  [per_device(): lax.all_gather(out_weight, 'ep', axis=1, tiled=True)]
    psum x1 -> x0, waiting for transfers between devices: 67.7 us -> none  [run_slots(): summed = lax.psum(gate_up.astype(jnp.bfloat16), 'tp').astype(jnp.float32)]
    all_gather x0 -> x2, waiting for transfers between devices: none -> 41.1 us  [the longest x1 29.3 us: gathered_experts(): rows = lax.all_gather(normed, 'ep', axis=0, tiled=True)]
    all_to_all x2 -> x0, other arithmetic: 30.3 us -> none  [the longest x1 15.5 us: relocate(): lax.all_to_all(outgoing, 'ep', split_axis=0, concat_axis=0, tiled=True)]
    all_to_all x6 -> x0, starting transfers between devices: 29.5 us -> none  [the longest x2 8.6 us: mix_block(): lax.all_to_all(outgoing, 'ep', split_axis=0, concat_axis=0, tiled=True)]
    unnamed x32 -> x19, local copies, waits for them, and re-layouts: 25.7 us -> 0.36 us
  transfers between devices with their start and end apart: 9 -> 6, of which waited for: 8 -> 6; matrix products, arithmetic and copies ran while one was open for 22% -> 6% of each run, Pallas kernels for 0% -> 0%
where the time goes in v1:
time: 283 us; the launch traced here: 282 us
  waiting for transfers between devices  204 us (72%)
  matrix products  31.6 us (11%)
  blocking collectives  19.9 us (7%)
  between operations  14.3 us (5%)
  other arithmetic  8.83 us (3%)
  local copies, waits for them, and re-layouts  3.12 us (1%)
    all_gather x1, waiting for transfers between devices, per_device(): lax.all_gather(out_weight, 'ep', axis=1, tiled=True)  70.5 us
    reduce_scatter x1, waiting for transfers between devices, gathered_experts(): lax.psum_scatter(gate_up, 'tp', scatter_dimension=0, tiled=True)  42.9 us
    reduce_scatter x1, waiting for transfers between devices, gathered_experts(): lax.psum_scatter(total.astype(jnp.bfloat16), 'ep', scatter_dimension=0, t...  36.2 us
    all_gather x1, waiting for transfers between devices, gathered_experts(): rows = lax.all_gather(normed, 'ep', axis=0, tiled=True)  29.3 us
    reduce_scatter x1, waiting for transfers between devices, per_device(): lax.psum_scatter(head_terms.astype(jnp.bfloat16), 'tp', scatter_dimension...  12.9 us
    all_gather x1, waiting for transfers between devices, gathered_experts(): hidden = lax.all_gather(hidden, 'tp', axis=0, tiled=True)  11.9 us
    all_to_all x1, blocking collectives, gathered_experts(): lax.all_to_all(by_slot.reshape(tokens_dev, groups, local_slots).transpose...  10 us
    dot_general x1, matrix products, gathered_experts(): jnp.einsum('rq,egqf->regf', rows, weights[:, :2], preferred_element_type=...  7.59 us
  transfers between devices with their start and end apart: 6, of which 6 were waited for; matrix products, arithmetic and copies ran while one was open for 6% of the time, Pallas kernels for 0%

profile of v1, /device:TPU:0, one launch (start us, length us, event | category | flops | bytes accessed | tf_op | source)
XLA Modules:
  0.0 282.4 jit_solution(5235431787822214977)
XLA Ops:
  6.5 0.0 copy-start
  6.5 0.0 copy-start.5
  6.5 0.0 copy-start.4
  6.5 0.0 all-gather.4.cloned.1.call-start
  6.5 0.7 all-gather.4.cloned.1.call-update
  7.3 0.0 reduce-scatter.4.cloned.1.call-start
  8.0 1.3 fusion.39
  9.2 0.2 copy.46
  9.4 0.3 copy.35
  9.7 0.0 copy-done.5
  9.7 0.1 copy.50
  9.8 0.0 copy-done.4
  9.9 0.4 fusion.40
  10.2 0.1 copy.32
  10.3 0.1 copy.33
  10.5 0.2 copy.31
  10.7 0.3 concatenate.23
  11.0 1.1 fusion.23
  12.1 6.1 %fusion.42 = (f32[2,8,128]{2,1,0:T(8,128)S(1)}, f32[2,8,128,1152]{2,3,1,0:T(8,128)}) fusion(pred[128,1152]{0,1:T(8,128)(4,1)S(1)} %fusion.23, bf16[128,2,8,128]{3,2,1,0:T(8,128)(2,1)S(1)} %bitcast.99, bf16[64,2,128]{2,0,1:T(8,128)(2,1)S(1)} %get-tuple-element.19, bf16[64,2,128]{2,0,1:T(8,128)(2,1)S(1)} %get-tuple-element.20, bf16[1024,2,128]{2,0,1:T(8,128)(2,1)S(1)} %copy.35), kind=kOutput, calls=%fused_computation.66 | convolution fusion | flops 617546880 | bytes 10706944 | tf_op jit(solution)/shard_map/sub | solution.py:45
  18.2 5.5 %fusion.16 = bf16[2,128,8,128]{3,1,2,0:T(8,128)(2,1)S(1)} fusion(f32[2,8,128,1152]{2,3,1,0:T(8,128)} %get-tuple-element.16, f32[2,8,128]{2,1,0:T(8,128)S(1)} %get-tuple-element.15, bf16[1152,2,128]{0,2,1:T(8,128)(2,1)S(1)} %concatenate.23), kind=kOutput, calls=%fused_computation.20 | convolution fusion | flops 608960512 | bytes 10559488 | tf_op jit(solution)/shard_map/qizo,oqx->zqix/dot_general | solution.py:47
  23.7 70.5 %all-gather.4.cloned.1.call-done = bf16[2048,2048]{1,0:T(8,128)(2,1)} async-done(((bf16[2048,256]{1,0:T(8,128)(2,1)}), bf16[2048,2048]{1,0:T(8,128)(2,1)}) %all-gather.4.cloned.1.call-update) | async-done | bytes 8388624 | tf_op jit(solution)/shard_map/all_gather | solution.py:158
  94.2 0.0 copy-start.1
  94.2 5.5 %convolution_convert_fusion = bf16[128,2048]{1,0:T(8,128)(2,1)} fusion(bf16[128,2048]{0,1:T(8,128)(2,1)S(1)} %bitcast.97, bf16[2048,2048]{1,0:T(8,128)(2,1)} %all-gather.4.cloned.1.call-done), kind=kOutput, calls=%fused_computation.12 | convolution fusion | flops 1074003968 | bytes 9437184 | tf_op jit(solution)/shard_map/dot_general | solution.py:156
  99.7 0.0 reduce-scatter.4.cloned.1.call-update
  99.7 0.0 all-gather.6.cloned.1.call-start
  99.7 12.9 %reduce-scatter.4.cloned.1.call-done = bf16[128,1024]{1,0:T(8,128)(2,1)} async-done(((bf16[128,2048]{1,0:T(8,128)(2,1)}), bf16[128,1024]{1,0:T(8,128)(2,1)}) %reduce-scatter.4.cloned.1.call-update) | async-done | bytes 262160 | tf_op jit(solution)/shard_map/reduce_scatter | solution.py:161
  112.7 0.0 copy-done.1
  112.7 1.1 fusion.24
  113.8 4.9 %psum.14 = f32[128]{0:T(128)S(1)} all-reduce(f32[128]{0:T(128)S(1)} %fusion.24), channel_id=1, replica_groups=mesh['rep'=2,'ep'=8,'tp'=2] {'tp'}, use_global_device_ids=true, to_apply=%region_5.6 | all-reduce | flops 128 | bytes 1024 | tf_op jit(solution)/shard_map/psum | solution.py:168
  118.7 1.8 fusion.25
  120.5 0.0 all-gather.6.cloned.1.call-update
  120.5 0.0 reduce-scatter.6.cloned.1.call-start
  120.5 29.3 %all-gather.6.cloned.1.call-done = bf16[1024,1024]{1,0:T(8,128)(2,1)} async-done(((bf16[128,1024]{1,0:T(8,128)(2,1)}), bf16[1024,1024]{1,0:T(8,128)(2,1)}) %all-gather.6.cloned.1.call-update) | async-done | bytes 2097168 | tf_op jit(solution)/shard_map/all_gather | solution.py:108
  149.8 7.6 %fusion.8 = bf16[1024,2,2,384]{3,0,2,1:T(8,128)(2,1)} fusion(bf16[2,3,1024,384]{3,2,1,0:T(8,128)(2,1)} %param.19, bf16[1024,1024]{1,0:T(8,128)(2,1)} %all-gather.6.cloned.1.call-done), kind=kOutput, calls=%fused_computation.13 | convolution fusion | flops 3222798336 | bytes 8388608 | tf_op jit(solution)/shard_map/rq,egqf->regf/dot_general | solution.py:116
  157.4 0.0 reduce-scatter.6.cloned.1.call-update
  157.4 0.0 copy-start.6
  157.4 0.0 copy-start.7
  157.5 0.0 copy-start.3
  157.5 0.0 all-gather.8.cloned.1.call-start
  157.5 42.9 %reduce-scatter.6.cloned.1.call-done = bf16[512,2,2,384]{3,0,2,1:T(8,128)(2,1)} async-done(((bf16[1024,2,2,384]{3,0,2,1:T(8,128)(2,1)}), bf16[512,2,2,384]{3,0,2,1:T(8,128)(2,1)}) %reduce-scatter.6.cloned.1.call-update) | async-done | bytes 1572880 | tf_op jit(solution)/shard_map/reduce_scatter | solution.py:119
  200.4 1.6 convert_element_type.84
  202.0 1.3 fusion.13
  203.4 0.0 all-gather.8.cloned.1.call-update
  203.4 0.0 reduce-scatter.8.cloned.1.call-start
  203.4 0.0 copy-done.6
  203.5 0.1 eq.14
  203.5 0.0 copy-done.7
  203.5 0.1 select_reduce_fusion.2
  203.6 0.0 copy-done
  203.6 0.0 copy-done.3
  203.6 0.2 convolution_convert_fusion.1
  203.8 4.9 %psum.15 = bf16[128,16]{0,1:T(8,128)(2,1)S(1)} all-reduce(bf16[128,16]{0,1:T(8,128)(2,1)S(1)} %convolution_convert_fusion.1), channel_id=1, replica_groups=mesh['rep'=2,'ep'=8,'tp'=2] {'tp'}, use_global_device_ids=true, to_apply=%region_6.7 | all-reduce | flops 2048 | bytes 8192 | tf_op jit(solution)/shard_map/psum | solution.py:170
  208.8 10.0 %all_to_all.5 = f32[8,128,2]{1,2,0:T(2,128)S(1)} all-to-all(f32[8,128,2]{1,2,0:T(2,128)S(1)} %bitcast.103), channel_id=1, replica_groups=mesh['rep'=2,'ep'=8,'tp'=2] {'ep'}, dimensions={0} | all-to-all | bytes 16384 | tf_op jit(solution)/shard_map/all_to_all | solution.py:109
  218.9 11.9 %all-gather.8.cloned.1.call-done = bf16[1024,2,384]{2,0,1:T(8,128)(2,1)} async-done(((bf16[512,2,384]{2,0,1:T(8,128)(2,1)}), bf16[1024,2,384]{2,0,1:T(8,128)(2,1)}) %all-gather.8.cloned.1.call-update) | async-done | bytes 1572880 | tf_op jit(solution)/shard_map/all_gather | solution.py:121
  230.7 2.6 fusion.17
  233.4 0.0 copy-start.2
  233.4 4.1 %add_convert_fusion = bf16[1024,1024]{1,0:T(8,128)(2,1)} fusion(f32[1024]{0:T(1024)S(1)} %bitcast.105, bf16[1024,1024]{1,0:T(8,128)(2,1)S(1)} %fusion.17, f32[1024]{0:T(1024)S(1)} %bitcast.104, bf16[1024,2,384]{2,0,1:T(8,128)(2,1)} %all-gather.8.cloned.1.call-done, bf16[2,3,1024,384]{3,2,1,0:T(8,128)(2,1)} %param.19), kind=kOutput, calls=%fused_computation.9 | convolution fusion | flops 812646400 | bytes 5775360 | tf_op jit(solution)/shard_map/dot_general | solution.py:124
  237.5 0.0 reduce-scatter.8.cloned.1.call-update
  237.5 36.2 %reduce-scatter.8.cloned.1.call-done = bf16[128,1024]{1,0:T(8,128)(2,1)} async-done(((bf16[1024,1024]{1,0:T(8,128)(2,1)}), bf16[128,1024]{1,0:T(8,128)(2,1)}) %reduce-scatter.8.cloned.1.call-update) | async-done | bytes 262160 | tf_op jit(solution)/shard_map/reduce_scatter | solution.py:128
  273.7 0.0 copy-done.2
  273.7 1.8 fusion.26
  (11 shorter events, 0.1 us)
Async XLA Ops:
  6.5 197.1 %copy-start = (bf16[1024,16]{0,1:T(8,128)(2,1)S(1)}, bf16[1024,16]{0,1:T(8,128)(2,1)}, u32[]{:S(2)}) copy-start(bf16[1024,16]{0,1:T(8,128)(2,1)} %param.18) | copy-start | bytes 98308
  6.5 3.2 %copy-start.5 = (bf16[2,64,2048]{2,1,0:T(8,128)(2,1)S(1)}, bf16[2,64,2048]{2,1,0:T(8,128)(2,1)}, u32[]{:S(2)}) copy-start(bf16[2,64,2048]{2,1,0:T(8,128)(2,1)} %param.13) | copy-start | bytes 1572868
  6.5 3.3 %copy-start.4 = (bf16[2,64,2,256]{3,2,1,0:T(2,128)(2,1)S(1)}, bf16[2,64,2,256]{3,2,1,0:T(2,128)(2,1)}, u32[]{:S(2)}) copy-start(bf16[2,64,2,256]{3,2,1,0:T(2,128)(2,1)} %param.14) | copy-start | bytes 393220
  6.5 87.6 %all-gather.4.cloned.1.call-start = ((), (), s32[]{:S(2)}) async-start(), calls=%async_computation.4 | async-start | bytes 9437184 | tf_op jit(solution)/shard_map/all_gather | solution.py:158
  7.3 105.4 %reduce-scatter.4.cloned.1.call-start = ((), (), s32[]{:S(2)}) async-start(), calls=%async_computation.5 | async-start | bytes 786432 | tf_op jit(solution)/shard_map/reduce_scatter | solution.py:161
  94.2 18.5 %copy-start.1 = (bf16[2,64,1024]{2,1,0:T(8,128)(2,1)S(1)}, bf16[2,64,1024]{2,1,0:T(8,128)(2,1)}, u32[]{:S(2)}) copy-start(bf16[2,64,1024]{2,1,0:T(8,128)(2,1)} %param.12) | copy-start | bytes 786436
  99.7 50.1 %all-gather.6.cloned.1.call-start = ((), (), s32[]{:S(2)}) async-start(), calls=%async_computation.6 | async-start | bytes 2359296 | tf_op jit(solution)/shard_map/all_gather | solution.py:108
  120.5 79.9 %reduce-scatter.6.cloned.1.call-start = ((), (), s32[]{:S(2)}) async-start(), calls=%async_computation.7 | async-start | bytes 4718592 | tf_op jit(solution)/shard_map/reduce_scatter | solution.py:119
  157.4 46.0 %copy-start.6 = (s32[2,64,8]{1,2,0:T(8,128)S(1)}, s32[2,64,8]{1,2,0:T(8,128)}, u32[]{:S(2)}) copy-start(s32[2,64,8]{1,2,0:T(8,128)} %param.20) | copy-start | bytes 12292
  157.4 46.1 %copy-start.7 = (s32[16]{0:T(128)S(1)}, s32[16]{0:T(128)}, u32[]{:S(2)}) copy-start(s32[16]{0:T(128)} %param.21) | copy-start | bytes 196
  157.5 46.2 %copy-start.3 = (bf16[128,1024]{1,0:T(8,128)(2,1)S(1)}, bf16[128,1024]{1,0:T(8,128)(2,1)}, u32[]{:S(2)}) copy-start(bf16[128,1024]{1,0:T(8,128)(2,1)} %fusion.25) | copy-start | bytes 786436
  157.5 73.2 %all-gather.8.cloned.1.call-start = ((), (), s32[]{:S(2)}) async-start(), calls=%async_computation.8 | async-start | bytes 2359296 | tf_op jit(solution)/shard_map/all_gather | solution.py:121
  203.4 70.4 %reduce-scatter.8.cloned.1.call-start = ((), (), s32[]{:S(2)}) async-start(), calls=%async_computation.9 | async-start | bytes 2359296 | tf_op jit(solution)/shard_map/reduce_scatter | solution.py:128
  233.4 40.4 %copy-start.2 = (bf16[128,1024]{1,0:T(8,128)(2,1)S(1)}, bf16[128,1024]{1,0:T(8,128)(2,1)}, u32[]{:S(2)}) copy-start(bf16[128,1024]{1,0:T(8,128)(2,1)} %reduce-scatter.4.cloned.1.call-done) | copy-start | bytes 786436
Sparse Core Ops, SparseCore 0:
  8.9 85.1 all-gather.3
  99.8 12.8 reduce-scatter.3
  120.6 29.1 all-gather.5
  157.6 42.8 reduce-scatter.5
  203.5 27.1 all-gather.7
  237.6 36.0 reduce-scatter.7

commit v2 on v1

--- a/solution.py
+++ b/solution.py
@@ -95,40 +95,88 @@
     return mixed_rows.astype(jnp.bfloat16)
 
 
-def gathered_experts(normed, resid, routed, combine, slot_table, weights):
-    tokens_dev, quarter = normed.shape
+def swap(value):
+    return lax.ppermute(value, "tp", [(0, 1), (1, 0)])
+
+
+def both_halves(value, axis):
+    other = swap(value)
+    first = lax.axis_index("tp") == 0
+    return jnp.concatenate(
+        [jnp.where(first, value, other), jnp.where(first, other, value)], axis
+    )
+
+
+def pick(table, index):
+    return lax.dynamic_index_in_dim(table, index, 0, keepdims=False)
+
+
+def gathered_layer(
+    attention, hidden_states, out_weight, router_weight, weights, routed, slot_table
+):
+    tokens_dev, width = attention.shape[0], hidden_states.shape[1]
     experts = slot_table.shape[0]
     local_slots = weights.shape[0]
     groups = lax.axis_size("ep")
-    slot_index = lookup(slot_table, routed)
-    slots = jnp.arange(experts, dtype=jnp.int32)
+    mine = lax.axis_index("tp")
+    theirs = 1 - mine
+    own_gate_up = pick(weights, mine)[:2]
+    sent_gate_up = swap(pick(weights, theirs)[:2])
+    first = mine == 0
+    gate_up_weight = jnp.concatenate(
+        [
+            jnp.where(first, own_gate_up, sent_gate_up),
+            jnp.where(first, sent_gate_up, own_gate_up),
+        ],
+        1,
+    )
+    hidden_full = both_halves(hidden_states, 1)
+    router_full = both_halves(router_weight, 0)
+    head_terms = jnp.dot(
+        attention,
+        lax.all_gather(out_weight, "ep", axis=1, tiled=True),
+        preferred_element_type=jnp.float32,
+    ).astype(jnp.bfloat16)
+    attn_out = head_terms.astype(jnp.float32) + swap(head_terms).astype(jnp.float32)
+    residual = (hidden_full.astype(jnp.float32) + attn_out).astype(jnp.bfloat16)
+    wide = residual.astype(jnp.float32)
+    squares = jnp.sum(wide * wide, 1)
+    normed = (wide * lax.rsqrt(squares / D + 1e-06)[:, None]).astype(jnp.bfloat16)
+    rows = lax.all_gather(normed, "ep", axis=0, tiled=True)
+    logits = jnp.dot(normed, router_full, preferred_element_type=jnp.float32)
+    slot_of = lookup(slot_table, routed)
+    marks = routed[:, :, None] == jnp.arange(experts, dtype=jnp.int32)
+    raised = jnp.where(marks.any(1), jnp.exp(logits), 0.0)
+    combine = raised / jnp.sum(raised, 1, keepdims=True)
+    picked = jnp.sum(jnp.where(marks, combine[:, None, :], 0.0), 2)
     by_slot = jnp.sum(
-        jnp.where(slot_index[:, :, None] == slots, combine[:, :, None], 0.0), 1
-    )
-    rows = lax.all_gather(normed, "ep", axis=0, tiled=True)
-    shares = lax.all_to_all(
-        by_slot.reshape(tokens_dev, groups, local_slots).transpose(1, 0, 2),
-        "ep",
-        split_axis=0,
-        concat_axis=0,
-        tiled=True,
-    ).reshape(groups * tokens_dev, local_slots)
-    gate_up = jnp.einsum(
-        "rq,egqf->regf", rows, weights[:, :2], preferred_element_type=jnp.float32
-    ).astype(jnp.bfloat16)
-    half = lax.psum_scatter(gate_up, "tp", scatter_dimension=0, tiled=True).astype(jnp.float32)
-    hidden = (jax.nn.silu(half[:, :, 0]) * half[:, :, 1]).astype(jnp.bfloat16)
-    hidden = lax.all_gather(hidden, "tp", axis=0, tiled=True)
-    total = 0.0
-    for slot in range(local_slots):
-        out = jnp.dot(
-            hidden[:, slot], weights[slot, 2].T, preferred_element_type=jnp.float32
-        ).astype(jnp.bfloat16)
-        total = total + shares[:, slot, None] * out.astype(jnp.float32)
+        jnp.where(
+            slot_of[:, :, None] == jnp.arange(experts, dtype=jnp.int32), picked[:, :, None], 0.0
+        ),
+        1,
+    )
+    shares = lax.all_gather(by_slot, "ep", axis=0, tiled=True)
+    local = jnp.arange(experts, dtype=jnp.int32)[None, :] - lax.axis_index("ep") * local_slots
+    own_share = jnp.sum(jnp.where(local == mine, shares, 0.0), 1, keepdims=True)
+    their_share = jnp.sum(jnp.where(local == theirs, shares, 0.0), 1, keepdims=True)
+    gate = jnp.dot(rows, gate_up_weight[0], preferred_element_type=jnp.float32)
+    up = jnp.dot(rows, gate_up_weight[1], preferred_element_type=jnp.float32)
+    hidden = (jax.nn.silu(gate) * up).astype(jnp.bfloat16)
+    their_hidden = swap(hidden)
+
+    def down(value, slot):
+        return lax.dot_general(
+            value, slot, (((1,), (1,)), ((), ())), preferred_element_type=jnp.float32
+        )
+
+    total = own_share * down(hidden, pick(weights, mine)[2]) + their_share * down(
+        their_hidden, pick(weights, theirs)[2]
+    )
     mixed = lax.psum_scatter(
         total.astype(jnp.bfloat16), "ep", scatter_dimension=0, tiled=True
     ).astype(jnp.float32)
-    return (resid.astype(jnp.float32) + mixed).astype(jnp.bfloat16)
+    own_residual = jnp.where(first, residual[:, :width], residual[:, width:])
+    return (own_residual.astype(jnp.float32) + mixed).astype(jnp.bfloat16)
 
 
 def per_device(
@@ -153,6 +201,22 @@
     local_slots = expert_weights.shape[0]
     capacity = min(tokens_dev, 3 * tokens_dev * top_count // (2 * experts))
     attention = attend_local(queries, fresh_key_value, cache, cache_lengths)
+    routed = expert_ids.reshape(2 * tokens_dev, top_count)
+    if (
+        tokens_dev <= local_slots * capacity
+        and lax.axis_size("tp") == 2
+        and local_slots == 2
+    ):
+        mixed = gathered_layer(
+            attention,
+            hidden_states.reshape(2 * tokens_dev, quarter),
+            out_weight,
+            router_weight,
+            expert_weights,
+            routed,
+            old_slots,
+        )
+        return mixed.reshape(2, tokens_dev, quarter)
     head_terms = jnp.dot(
         attention,
         lax.all_gather(out_weight, "ep", axis=1, tiled=True),
@@ -171,7 +235,6 @@
         jnp.dot(normed, router_weight, preferred_element_type=jnp.float32).astype(jnp.bfloat16),
         "tp",
     ).astype(jnp.float32)
-    routed = expert_ids.reshape(2 * tokens_dev, top_count)
     selected = jnp.sum(
         jnp.where(
             routed[:, :, None] == jnp.arange(experts, dtype=jnp.int32)[None, None, :],
@@ -182,9 +245,6 @@
     )
     raised = jnp.exp(selected)
     combine = raised / jnp.sum(raised, 1, keepdims=True)
-    if groups * tokens_dev <= groups * local_slots * capacity:
-        mixed = gathered_experts(normed, residual, routed, combine, old_slots, expert_weights)
-        return mixed.reshape(2, tokens_dev, quarter)
     outputs = []
     for lower in (0, tokens_dev):
         upper = lower + tokens_dev

time: 283 us -> 240 us (0.85)
  waiting for transfers between devices: 204 us -> 163 us
  blocking collectives: 19.9 us -> 14.1 us
  starting transfers between devices: 0.21 us -> 5.8 us
    reduce_scatter x3 -> x1, waiting for transfers between devices: 92 us -> 35 us  [gathered_layer(): lax.psum_scatter(total.astype(jnp.bfloat16), 'ep', scatter_dimension=0, t...]
    ppermute x0 -> x5, waiting for transfers between devices: none -> 53.3 us  [swap(): return lax.ppermute(value, 'tp', [(0, 1), (1, 0)])]
    all_gather x3 -> x2, waiting for transfers between devices: 112 us -> 73.9 us  [the longest x1 70.5 us: gathered_layer(): lax.all_gather(out_weight, 'ep', axis=1, tiled=True)]
    all_gather x0 -> x1, blocking collectives: none -> 14.1 us  [gathered_layer(): shares = lax.all_gather(by_slot, 'ep', axis=0, tiled=True)]
    all_to_all x1 -> x0, blocking collectives: 10 us -> none  [gathered_experts(): lax.all_to_all(by_slot.reshape(tokens_dev, groups, local_slots).transpose...]
    psum x2 -> x0, blocking collectives: 9.86 us -> none  [the longest x1 4.93 us: per_device(): lax.psum(jnp.dot(normed, router_weight, preferred_element_type=jnp.float3...]
    ppermute x0 -> x5, starting transfers between devices: none -> 5.71 us  [swap(): return lax.ppermute(value, 'tp', [(0, 1), (1, 0)])]
    convert_element_type x5 -> x2, other arithmetic: 6.48 us -> 2.74 us  [the longest x1 1.78 us: gathered_layer(): return (own_residual.astype(jnp.float32) + mixed).astype(jnp.bfloat16)]
  transfers between devices with their start and end apart: 6 -> 8, of which waited for: 6 -> 6; matrix products, arithmetic and copies ran while one was open for 6% -> 10% of each run, Pallas kernels for 0% -> 0%
where the time goes in v2:
time: 240 us
  waiting for transfers between devices  163 us (68%)
  matrix products  30.1 us (13%)
  blocking collectives  14.1 us (6%)
  between operations  14 us (6%)
  other arithmetic  7.91 us (3%)
  starting transfers between devices  5.8 us (2%)
  local copies, waits for them, and re-layouts  4.69 us (2%)
    all_gather x1, waiting for transfers between devices, gathered_layer(): lax.all_gather(out_weight, 'ep', axis=1, tiled=True)  70.5 us
    ppermute x5, waiting for transfers between devices, swap(): return lax.ppermute(value, 'tp', [(0, 1), (1, 0)])  53.3 us
    reduce_scatter x1, waiting for transfers between devices, gathered_layer(): lax.psum_scatter(total.astype(jnp.bfloat16), 'ep', scatter_dimension=0, t...  35 us
    all_gather x1, blocking collectives, gathered_layer(): shares = lax.all_gather(by_slot, 'ep', axis=0, tiled=True)  14.1 us
    dot_general x2, matrix products, down(): lax.dot_general(value, slot, (((1,), (1,)), ((), ())), preferred_element_...  6.23 us
    sub x1, matrix products, attend_local(): attention_scores - largest  6.12 us
    ppermute x5, starting transfers between devices, swap(): return lax.ppermute(value, 'tp', [(0, 1), (1, 0)])  5.71 us
    dot_general x1, matrix products, attend_local(): jnp.einsum('qizo,oqx->zqix', route_probability, value_matrix.reshape(key_...  5.46 us
  transfers between devices with their start and end apart: 8, of which 6 were waited for; matrix products, arithmetic and copies ran while one was open for 10% of the time, Pallas kernels for 0%

profile of v2, /device:TPU:0, one launch (start us, length us, event | category | flops | bytes accessed | tf_op | source)
XLA Modules:
  0.0 239.5 jit_solution(15800710076072277968)
XLA Ops:
  6.5 0.0 copy-start.3
  6.5 0.0 copy-start.2
  6.5 0.0 all-gather.3.cloned.1.call-start
  6.5 0.7 all-gather.3.cloned.1.call-update
  7.3 0.0 all-gather.5.cloned.1.call-start
  8.0 1.3 fusion.54
  9.2 0.2 copy.42
  9.4 0.3 copy.33
  9.7 0.0 copy-done.3
  9.7 0.1 copy.45
  9.8 0.0 copy-done.2
  9.9 0.4 fusion.55
  10.2 0.1 copy.30
  10.3 0.1 copy.31
  10.5 0.2 copy.29
  10.7 0.3 concatenate.33
  11.0 1.1 fusion.24
  12.1 6.1 %fusion.56 = (f32[2,8,128]{2,1,0:T(8,128)S(1)}, f32[2,8,128,1152]{2,3,1,0:T(8,128)}) fusion(pred[128,1152]{0,1:T(8,128)(4,1)S(1)} %fusion.24, bf16[128,2,8,128]{3,2,1,0:T(8,128)(2,1)S(1)} %bitcast.83, bf16[64,2,128]{2,0,1:T(8,128)(2,1)S(1)} %get-tuple-element.29, bf16[64,2,128]{2,0,1:T(8,128)(2,1)S(1)} %get-tuple-element.30, bf16[1024,2,128]{2,0,1:T(8,128)(2,1)S(1)} %copy.33), kind=kOutput, calls=%fused_computation.90 | convolution fusion | flops 617546880 | bytes 10706944 | tf_op jit(solution)/shard_map/sub | solution.py:45
  18.2 5.5 %fusion.17 = bf16[2,128,8,128]{3,1,2,0:T(8,128)(2,1)S(1)} fusion(f32[2,8,128,1152]{2,3,1,0:T(8,128)} %get-tuple-element.24, f32[2,8,128]{2,1,0:T(8,128)S(1)} %get-tuple-element.23, bf16[1152,2,128]{0,2,1:T(8,128)(2,1)S(1)} %concatenate.33), kind=kOutput, calls=%fused_computation.29 | convolution fusion | flops 608960512 | bytes 10559488 | tf_op jit(solution)/shard_map/qizo,oqx->zqix/dot_general | solution.py:47
  23.7 70.5 %all-gather.3.cloned.1.call-done = bf16[2048,2048]{1,0:T(8,128)(2,1)} async-done(((bf16[2048,256]{1,0:T(8,128)(2,1)}), bf16[2048,2048]{1,0:T(8,128)(2,1)}) %all-gather.3.cloned.1.call-update) | async-done | bytes 8388624 | tf_op jit(solution)/shard_map/all_gather | solution.py:137
  94.2 0.0 copy-start.4
  94.2 4.7 %convolution_convert_fusion = bf16[128,2048]{1,0:T(8,128)(2,1)S(1)} fusion(bf16[128,2048]{0,1:T(8,128)(2,1)S(1)} %bitcast.81, bf16[2048,2048]{1,0:T(8,128)(2,1)} %all-gather.3.cloned.1.call-done), kind=kOutput, calls=%fused_computation.13 | convolution fusion | flops 1074003968 | bytes 9437184 | tf_op jit(solution)/shard_map/dot_general | solution.py:135
  98.9 1.5 collective-permute-start.1
  100.4 0.0 copy-done.4
  100.4 0.6 collective-permute-start
  101.0 17.7 %collective-permute-done = bf16[128,1024]{1,0:T(8,128)(2,1)S(1)} collective-permute-done((bf16[128,1024]{1,0:T(8,128)(2,1)S(1)}, bf16[128,1024]{1,0:T(8,128)(2,1)S(1)}, u32[]{:S(2)}, u32[]{:S(2)}) %collective-permute-start) | collective-permute-done | bytes 262176 | tf_op jit(solution)/shard_map/ppermute | solution.py:99
  118.6 0.1 broadcast_select_fusion.3
  118.7 0.0 collective-permute-done.1
  118.7 0.0 copy-start.5
  118.7 0.0 copy-start.6
  118.7 0.0 copy-start.7
  118.7 0.4 fusion.20
  119.1 1.0 fusion.21
  120.1 0.0 all-gather.5.cloned.1.call-update
  120.1 0.0 reduce-scatter.2.cloned.1.call-start
  120.2 1.6 dynamic-slice_bitcast_fusion
  121.7 1.5 collective-permute-start.3
  123.3 0.0 copy-done.5
  123.3 0.6 collective-permute-start.2
  123.8 0.0 copy-done.6
  123.8 0.1 eq.65
  123.9 0.0 copy-done.7
  123.9 0.1 select_reduce_fusion.3
  124.1 34.1 %collective-permute-done.2 = bf16[1024,16]{0,1:T(8,128)(2,1)S(1)} collective-permute-done((bf16[1024,16]{0,1:T(8,128)(2,1)S(1)}, bf16[1024,16]{0,1:T(8,128)(2,1)S(1)}, u32[]{:S(2)}, u32[]{:S(2)}) %collective-permute-start.2) | collective-permute-done | bytes 32800 | tf_op jit(solution)/shard_map/ppermute | solution.py:99
  158.2 0.0 copy-start
  158.2 0.0 collective-permute-done.3
  158.2 3.4 %broadcast_select_fusion = (bf16[2,1024,384]{2,1,0:T(8,128)(2,1)S(1)}, bf16[2,1024,384]{2,1,0:T(8,128)(2,1)}) fusion(bf16[2,1024,384]{2,1,0:T(8,128)(2,1)} %collective-permute-done.3, pred[]{:T(512)S(6)} %eq.62, bf16[2,3,1024,384]{3,2,1,0:T(8,128)(2,1)} %param.19, s32[]{:T(128)S(6)} %select_n.99), kind=kLoop, calls=%fused_computation.24 | loop fusion | flops 1572864 | bytes 6291461 | tf_op jit(solution)/shard_map/jit(_where)/select_n | solution.py:129
  161.7 0.0 copy-done
  161.7 0.3 fusion.59
  161.9 3.4 %all-gather.5.cloned.1.call-done = bf16[1024,2048]{1,0:T(8,128)(2,1)} async-done(((bf16[128,2048]{1,0:T(8,128)(2,1)}), bf16[1024,2048]{1,0:T(8,128)(2,1)}) %all-gather.5.cloned.1.call-update) | async-done | bytes 4194320 | tf_op jit(solution)/shard_map/all_gather | solution.py:145
  165.3 0.0 copy-start.1
  165.4 4.9 %fusion.9 = f32[1024,384]{1,0:T(8,128)S(1)} fusion(bf16[1024,2048]{1,0:T(8,128)(2,1)} %all-gather.5.cloned.1.call-done, bf16[2,1024,384]{2,1,0:T(8,128)(2,1)} %get-tuple-element.12, bf16[2,1024,384]{2,1,0:T(8,128)(2,1)S(1)} %get-tuple-element.11), kind=kOutput, calls=%fused_computation.16 | convolution fusion | flops 1613758464 | bytes 8912896 | tf_op jit(solution)/shard_map/dot_general | solution.py:162
  170.2 0.0 copy-done.1
  170.2 0.0 copy-done.8
  170.2 2.4 %multiply_convert_fusion = bf16[1024,384]{1,0:T(8,128)(2,1)S(1)} fusion(f32[1024,384]{1,0:T(8,128)S(1)} %fusion.9, bf16[1024,2048]{1,0:T(8,128)(2,1)S(1)} %copy-done.8, bf16[2,1024,384]{2,1,0:T(8,128)(2,1)S(1)} %get-tuple-element.11, bf16[2,1024,384]{2,1,0:T(8,128)(2,1)S(1)} %copy-done.1), kind=kOutput, calls=%fused_computation.23 | convolution fusion | flops 1616117760 | bytes 9699328 | tf_op jit(solution)/shard_map/dot_general | solution.py:163
  172.7 1.5 collective-permute-start.4
  174.2 14.1 %all_gather.10 = f32[1024,16]{0,1:T(8,128)S(1)} all-gather(f32[128,16]{0,1:T(8,128)S(1)} %fusion.60), channel_id=1, replica_groups=mesh['rep'=2,'ep'=8,'tp'=2] {'ep'}, dimensions={0}, use_global_device_ids=true | all-gather | bytes 73728 | tf_op jit(solution)/shard_map/all_gather | solution.py:158
  188.4 0.1 select_reduce_fusion.2
  188.5 2.4 %fusion.22 = f32[1024,1024]{1,0:T(8,128)S(1)} fusion(bf16[1024,384]{1,0:T(8,128)(2,1)S(1)} %multiply_convert_fusion, bf16[2,3,1024,384]{3,2,1,0:T(8,128)(2,1)} %param.19, s32[]{:T(128)S(6)} %select_n.99, s32[]{:T(128)S(6)} %add.55), kind=kOutput, calls=%fused_computation.38 | convolution fusion | flops 805306368 | bytes 5767176 | tf_op jit(solution)/shard_map/dot_general | solution.py:168
  190.9 1.5 collective-permute-done.4
  192.4 3.8 %add_convert_fusion = bf16[1024,1024]{1,0:T(8,128)(2,1)} fusion(f32[1024,1024]{1,0:T(8,128)S(1)} %fusion.22, bf16[1024,384]{1,0:T(8,128)(2,1)S(1)} %collective-permute-done.4, f32[1024]{0:T(1024)S(1)} %get-tuple-element.8, f32[1024]{0:T(1024)S(1)} %get-tuple-element.7, bf16[2,3,1024,384]{3,2,1,0:T(8,128)(2,1)} %param.19, s32[]{:T(128)S(6)} %select_n.100, ...), kind=kOutput, calls=%fused_computation.10 | convolution fusion | flops 809500672 | bytes 7872520 | tf_op jit(solution)/shard_map/dot_general | solution.py:168
  196.2 0.0 reduce-scatter.2.cloned.1.call-update
  196.3 35.0 %reduce-scatter.2.cloned.1.call-done = bf16[128,1024]{1,0:T(8,128)(2,1)} async-done(((bf16[1024,1024]{1,0:T(8,128)(2,1)}), bf16[128,1024]{1,0:T(8,128)(2,1)}) %reduce-scatter.2.cloned.1.call-update) | async-done | bytes 262160 | tf_op jit(solution)/shard_map/reduce_scatter | solution.py:175
  231.2 1.8 add_convert_fusion.2
  (12 shorter events, 0.1 us)
Async XLA Ops:
  6.5 3.2 %copy-start.3 = (bf16[2,64,2048]{2,1,0:T(8,128)(2,1)S(1)}, bf16[2,64,2048]{2,1,0:T(8,128)(2,1)}, u32[]{:S(2)}) copy-start(bf16[2,64,2048]{2,1,0:T(8,128)(2,1)} %param.13) | copy-start | bytes 1572868
  6.5 3.3 %copy-start.2 = (bf16[2,64,2,256]{3,2,1,0:T(2,128)(2,1)S(1)}, bf16[2,64,2,256]{3,2,1,0:T(2,128)(2,1)}, u32[]{:S(2)}) copy-start(bf16[2,64,2,256]{3,2,1,0:T(2,128)(2,1)} %param.14) | copy-start | bytes 393220
  6.5 87.6 %all-gather.3.cloned.1.call-start = ((), (), s32[]{:S(2)}) async-start(), calls=%async_computation.1 | async-start | bytes 9437184 | tf_op jit(solution)/shard_map/all_gather | solution.py:137
  7.3 158.1 %all-gather.5.cloned.1.call-start = ((), (), s32[]{:S(2)}) async-start(), calls=%async_computation.2 | async-start | bytes 4718592 | tf_op jit(solution)/shard_map/all_gather | solution.py:145
  94.2 6.3 %copy-start.4 = (bf16[2,64,1024]{2,1,0:T(8,128)(2,1)S(1)}, bf16[2,64,1024]{2,1,0:T(8,128)(2,1)}, u32[]{:S(2)}) copy-start(bf16[2,64,1024]{2,1,0:T(8,128)(2,1)} %param.12) | copy-start | bytes 786436
  98.9 19.8 %collective-permute-start.1 = (bf16[128,2048]{1,0:T(8,128)(2,1)S(1)}, bf16[128,2048]{1,0:T(8,128)(2,1)S(1)}, u32[]{:S(2)}, u32[]{:S(2)}) collective-permute-start(bf16[128,2048]{1,0:T(8,128)(2,1)S(1)} %convolution_convert_fusion), channel_id=1, source_target_pairs={{0,1},{1,0},{2,3},{3,2},{4,5},{5,4},{6,7},{7,6},{8,9},{9,8},{10,11... | collective-permute-start | bytes 1572872 | tf_op jit(solution)/shard_map/ppermute | solution.py:99
  100.4 18.2 %collective-permute-start = (bf16[128,1024]{1,0:T(8,128)(2,1)S(1)}, bf16[128,1024]{1,0:T(8,128)(2,1)S(1)}, u32[]{:S(2)}, u32[]{:S(2)}) collective-permute-start(bf16[128,1024]{1,0:T(8,128)(2,1)S(1)} %bitcast.86), channel_id=1, source_target_pairs={{0,1},{1,0},{2,3},{3,2},{4,5},{5,4},{6,7},{7,6},{8,9},{9,8},{10,11... | collective-permute-start | bytes 786440 | tf_op jit(solution)/shard_map/ppermute | solution.py:99
  118.7 4.6 %copy-start.5 = (bf16[1024,16]{0,1:T(8,128)(2,1)S(1)}, bf16[1024,16]{0,1:T(8,128)(2,1)}, u32[]{:S(2)}) copy-start(bf16[1024,16]{0,1:T(8,128)(2,1)} %param.18) | copy-start | bytes 98308
  118.7 5.1 %copy-start.6 = (s32[2,64,8]{1,2,0:T(8,128)S(1)}, s32[2,64,8]{1,2,0:T(8,128)}, u32[]{:S(2)}) copy-start(s32[2,64,8]{1,2,0:T(8,128)} %param.20) | copy-start | bytes 12292
  118.7 5.2 %copy-start.7 = (s32[16]{0:T(128)S(1)}, s32[16]{0:T(128)}, u32[]{:S(2)}) copy-start(s32[16]{0:T(128)} %param.21) | copy-start | bytes 196
  120.1 111.1 %reduce-scatter.2.cloned.1.call-start = ((), (), s32[]{:S(2)}) async-start(), calls=%async_computation.3 | async-start | bytes 2359296 | tf_op jit(solution)/shard_map/reduce_scatter | solution.py:175
  121.7 36.5 %collective-permute-start.3 = (bf16[2,1024,384]{2,1,0:T(8,128)(2,1)S(1)}, bf16[2,1024,384]{2,1,0:T(8,128)(2,1)}, u32[]{:S(2)}, u32[]{:S(2)}) collective-permute-start(bf16[2,1024,384]{2,1,0:T(8,128)(2,1)S(1)} %dynamic-slice_bitcast_fusion), channel_id=1, source_target_pairs={{0,1},{1,0},{2,3},{3,2},{4,5},{5,4},{6,7},{7,6},{8,9},{9,8},{10,11... | collective-permute-start | bytes 4718600 | tf_op jit(solution)/shard_map/ppermute | solution.py:99
  123.3 34.9 %collective-permute-start.2 = (bf16[1024,16]{0,1:T(8,128)(2,1)S(1)}, bf16[1024,16]{0,1:T(8,128)(2,1)S(1)}, u32[]{:S(2)}, u32[]{:S(2)}) collective-permute-start(bf16[1024,16]{0,1:T(8,128)(2,1)S(1)} %copy-done.5), channel_id=1, source_target_pairs={{0,1},{1,0},{2,3},{3,2},{4,5},{5,4},{6,7},{7,6},{8,9},{9,8},{10,11... | collective-permute-start | bytes 98312 | tf_op jit(solution)/shard_map/ppermute | solution.py:99
  158.2 3.5 %copy-start = (bf16[128,2048]{1,0:T(8,128)(2,1)S(1)}, bf16[128,2048]{1,0:T(8,128)(2,1)}, u32[]{:S(2)}) copy-start(bf16[128,2048]{1,0:T(8,128)(2,1)} %fusion.21) | copy-start | bytes 1572868
  165.3 4.9 %copy-start.1 = (bf16[2,1024,384]{2,1,0:T(8,128)(2,1)S(1)}, bf16[2,1024,384]{2,1,0:T(8,128)(2,1)}, u32[]{:S(2)}) copy-start(bf16[2,1024,384]{2,1,0:T(8,128)(2,1)} %get-tuple-element.12) | copy-start | bytes 4718596
  165.3 4.9 %copy-start.8 = (bf16[1024,2048]{1,0:T(8,128)(2,1)S(1)}, bf16[1024,2048]{1,0:T(8,128)(2,1)}, u32[]{:S(2)}) copy-start(bf16[1024,2048]{1,0:T(8,128)(2,1)} %all-gather.5.cloned.1.call-done) | copy-start | bytes 12582916
  172.7 19.7 %collective-permute-start.4 = (bf16[1024,384]{1,0:T(8,128)(2,1)S(1)}, bf16[1024,384]{1,0:T(8,128)(2,1)S(1)}, u32[]{:S(2)}, u32[]{:S(2)}) collective-permute-start(bf16[1024,384]{1,0:T(8,128)(2,1)S(1)} %multiply_convert_fusion), channel_id=1, source_target_pairs={{0,1},{1,0},{2,3},{3,2},{4,5},{5,4},{6,7},{7,6},{8,9},{9,8},{10,11... | collective-permute-start | bytes 2359304 | tf_op jit(solution)/shard_map/ppermute | solution.py:99
Sparse Core Ops, SparseCore 0:
  8.9 85.1 all-gather.2
  120.2 45.0 all-gather.4
  196.4 34.8 reduce-scatter.1

commit v3 on v2

--- a/solution.py
+++ b/solution.py
@@ -5,6 +5,8 @@
 
 D = 2048
 HEAD_SIZE = 128
+PIECES = 2
+CHUNKS = 2
 
 
 def lookup(entries, wanted_keys):
@@ -132,49 +134,61 @@
     )
     hidden_full = both_halves(hidden_states, 1)
     router_full = both_halves(router_weight, 0)
-    head_terms = jnp.dot(
-        attention,
-        lax.all_gather(out_weight, "ep", axis=1, tiled=True),
-        preferred_element_type=jnp.float32,
-    ).astype(jnp.bfloat16)
-    attn_out = head_terms.astype(jnp.float32) + swap(head_terms).astype(jnp.float32)
+    routed_all = lax.all_gather(routed, "ep", axis=0)
+    attention, gate_up_weight, hidden_full, router_full, routed_all = lax.optimization_barrier(
+        (attention, gate_up_weight, hidden_full, router_full, routed_all)
+    )
+    slots = jnp.arange(experts, dtype=jnp.int32)
+    marks = (routed_all[:, :, :, None] == slots).any(2)
+    base_slot = lax.axis_index("ep") * local_slots
+    columns = out_weight.shape[1] // PIECES
+    parts = []
+    for piece in range(PIECES):
+        block = lax.all_gather(
+            out_weight[:, piece * columns : (piece + 1) * columns], "ep", axis=1, tiled=True
+        )
+        terms = jnp.dot(attention, block, preferred_element_type=jnp.float32).astype(jnp.bfloat16)
+        summed = terms.astype(jnp.float32) + swap(terms).astype(jnp.float32)
+        parts.append(summed.reshape(tokens_dev, groups, columns))
+    attn_out = jnp.stack(parts, 2).reshape(tokens_dev, 2 * width)
     residual = (hidden_full.astype(jnp.float32) + attn_out).astype(jnp.bfloat16)
     wide = residual.astype(jnp.float32)
     squares = jnp.sum(wide * wide, 1)
     normed = (wide * lax.rsqrt(squares / D + 1e-06)[:, None]).astype(jnp.bfloat16)
-    rows = lax.all_gather(normed, "ep", axis=0, tiled=True)
-    logits = jnp.dot(normed, router_full, preferred_element_type=jnp.float32)
-    slot_of = lookup(slot_table, routed)
-    marks = routed[:, :, None] == jnp.arange(experts, dtype=jnp.int32)
-    raised = jnp.where(marks.any(1), jnp.exp(logits), 0.0)
-    combine = raised / jnp.sum(raised, 1, keepdims=True)
-    picked = jnp.sum(jnp.where(marks, combine[:, None, :], 0.0), 2)
-    by_slot = jnp.sum(
-        jnp.where(
-            slot_of[:, :, None] == jnp.arange(experts, dtype=jnp.int32), picked[:, :, None], 0.0
-        ),
-        1,
-    )
-    shares = lax.all_gather(by_slot, "ep", axis=0, tiled=True)
-    local = jnp.arange(experts, dtype=jnp.int32)[None, :] - lax.axis_index("ep") * local_slots
-    own_share = jnp.sum(jnp.where(local == mine, shares, 0.0), 1, keepdims=True)
-    their_share = jnp.sum(jnp.where(local == theirs, shares, 0.0), 1, keepdims=True)
-    gate = jnp.dot(rows, gate_up_weight[0], preferred_element_type=jnp.float32)
-    up = jnp.dot(rows, gate_up_weight[1], preferred_element_type=jnp.float32)
-    hidden = (jax.nn.silu(gate) * up).astype(jnp.bfloat16)
-    their_hidden = swap(hidden)
-
+    chunk = tokens_dev // CHUNKS
+    gathered = [
+        lax.all_gather(normed[lower : lower + chunk], "ep", axis=0, tiled=True)
+        for lower in range(0, tokens_dev, chunk)
+    ]
     def down(value, slot):
         return lax.dot_general(
             value, slot, (((1,), (1,)), ((), ())), preferred_element_type=jnp.float32
         )
 
-    total = own_share * down(hidden, pick(weights, mine)[2]) + their_share * down(
-        their_hidden, pick(weights, theirs)[2]
-    )
-    mixed = lax.psum_scatter(
-        total.astype(jnp.bfloat16), "ep", scatter_dimension=0, tiled=True
-    ).astype(jnp.float32)
+    own_down = pick(weights, mine)[2]
+    their_down = pick(weights, theirs)[2]
+    mixed = []
+    for index, rows in enumerate(gathered):
+        span = slice(index * chunk, (index + 1) * chunk)
+        gate = jnp.dot(rows, gate_up_weight[0], preferred_element_type=jnp.float32)
+        up = jnp.dot(rows, gate_up_weight[1], preferred_element_type=jnp.float32)
+        hidden = (jax.nn.silu(gate) * up).astype(jnp.bfloat16)
+        their_hidden = swap(hidden)
+        logits = jnp.dot(rows, router_full, preferred_element_type=jnp.float32)
+        raised = jnp.where(marks[:, span].reshape(-1, experts), jnp.exp(logits), 0.0)
+        combine = raised / jnp.sum(raised, 1, keepdims=True)
+        own_share = jnp.sum(
+            jnp.where(slot_table == base_slot + mine, combine, 0.0), 1, keepdims=True
+        )
+        their_share = jnp.sum(
+            jnp.where(slot_table == base_slot + theirs, combine, 0.0), 1, keepdims=True
+        )
+        total = own_share * down(hidden, own_down) + their_share * down(their_hidden, their_down)
+        total = total.astype(jnp.bfloat16)
+        if index + 1 < len(gathered):
+            total, gathered[index + 1] = lax.optimization_barrier((total, gathered[index + 1]))
+        mixed.append(lax.psum_scatter(total, "ep", scatter_dimension=0, tiled=True))
+    mixed = jnp.concatenate(mixed, 0).astype(jnp.float32)
     own_residual = jnp.where(first, residual[:, :width], residual[:, width:])
     return (own_residual.astype(jnp.float32) + mixed).astype(jnp.bfloat16)
 

time: 240 us -> 256 us (1.067)
  waiting for transfers between devices: 163 us -> 156 us
  matrix products: 30.1 us -> 37 us
  starting transfers between devices: 5.8 us -> 11.8 us
  local copies, waits for them, and re-layouts: 4.69 us -> 10.5 us
  blocking collectives: 14.1 us -> 17.6 us
    ppermute x5 -> x7, waiting for transfers between devices: 53.3 us -> 27.6 us  [swap(): return lax.ppermute(value, 'tp', [(0, 1), (1, 0)])]
    reduce_scatter x1 -> x2, waiting for transfers between devices: 35 us -> 47.8 us  [gathered_layer(): mixed.append(lax.psum_scatter(total, 'ep', scatter_dimension=0, tiled=True))]
    ppermute x5 -> x7, starting transfers between devices: 5.71 us -> 11.4 us  [swap(): return lax.ppermute(value, 'tp', [(0, 1), (1, 0)])]
    all_gather x2 -> x4, waiting for transfers between devices: 73.9 us -> 79.2 us  [the longest x2 42 us: gathered_layer(): lax.all_gather(out_weight[:, piece * columns:(piece + 1) * columns], 'ep'...]
    all_gather x1, blocking collectives: 14.1 us -> 17.6 us  [gathered_layer(): routed_all = lax.all_gather(routed, 'ep', axis=0)]
    dot_general x2 -> x4, matrix products: 6.23 us -> 9.55 us  [down(): lax.dot_general(value, slot, (((1,), (1,)), ((), ())), preferred_element_...]
    slice x0 -> x5, local copies, waits for them, and re-layouts: none -> 3.17 us  [the longest x1 2.24 us: gathered_layer(): out_weight[:, piece * columns:(piece + 1) * columns]]
    dot_general x2 -> x4, matrix products: 4.97 us -> 7.2 us  [the longest x2 5.84 us: gathered_layer(): jnp.dot(attention, block, preferred_element_type=jnp.float32)]
  transfers between devices with their start and end apart: 8 -> 13, of which waited for: 6 -> 9; matrix products, arithmetic and copies ran while one was open for 10% -> 19% of each run, Pallas kernels for 0% -> 0%
where the time goes in v3:
time: 256 us; the launch traced here: 255 us
  waiting for transfers between devices  156 us (61%)
  matrix products  37 us (14%)
  blocking collectives  17.6 us (7%)
  between operations  14.6 us (6%)
  starting transfers between devices  11.8 us (5%)
  local copies, waits for them, and re-layouts  10.5 us (4%)
  other arithmetic  7.95 us (3%)
    reduce_scatter x2, waiting for transfers between devices, gathered_layer(): mixed.append(lax.psum_scatter(total, 'ep', scatter_dimension=0, tiled=True))  47.8 us
    all_gather x2, waiting for transfers between devices, gathered_layer(): lax.all_gather(out_weight[:, piece * columns:(piece + 1) * columns], 'ep'...  42 us
    all_gather x2, waiting for transfers between devices, gathered_layer(): lax.all_gather(normed[lower:lower + chunk], 'ep', axis=0, tiled=True)  37.3 us
    ppermute x7, waiting for transfers between devices, swap(): return lax.ppermute(value, 'tp', [(0, 1), (1, 0)])  27.6 us
    all_gather x1, blocking collectives, gathered_layer(): routed_all = lax.all_gather(routed, 'ep', axis=0)  17.6 us
    ppermute x7, starting transfers between devices, swap(): return lax.ppermute(value, 'tp', [(0, 1), (1, 0)])  11.4 us
    dot_general x4, matrix products, down(): lax.dot_general(value, slot, (((1,), (1,)), ((), ())), preferred_element_...  9.55 us
    dot_general x2, matrix products, gathered_layer(): gate = jnp.dot(rows, gate_up_weight[0], preferred_element_type=jnp.float32)  6.86 us
  transfers between devices with their start and end apart: 13, of which 9 were waited for; matrix products, arithmetic and copies ran while one was open for 19% of the time, Pallas kernels for 0%

profile of v3, /device:TPU:0, one launch (start us, length us, event | category | flops | bytes accessed | tf_op | source)
XLA Modules:
  0.0 255.3 jit_solution(7172595248650627875)
XLA Ops:
  6.5 2.2 fusion.57
  8.9 0.7 all-gather.5.cloned.1.call-update
  9.6 2.8 %dynamic-slice_bitcast_fusion = bf16[2,1024,384]{2,1,0:T(8,128)(2,1)} fusion(bf16[2,3,1024,384]{3,2,1,0:T(8,128)(2,1)} %param.19, s32[]{:T(128)S(6)} %select_n.86), kind=kLoop, calls=%fused_computation.12 | loop fusion | bytes 3145732 | tf_op jit(solution)/shard_map/slice | solution.py:126
  12.5 3.0 %collective-permute-start = (bf16[2,1024,384]{2,1,0:T(8,128)(2,1)}, bf16[2,1024,384]{2,1,0:T(8,128)(2,1)}, u32[]{:S(2)}, u32[]{:S(2)}) collective-permute-start(bf16[2,1024,384]{2,1,0:T(8,128)(2,1)} %dynamic-slice_bitcast_fusion), channel_id=1, source_target_pairs={{0,1},{1,0},{2,3},{3,2},{4,5},{5,4},{6,7},{7,6},{8,9},{9,8},{10,11... | collective-permute-start | bytes 4718600 | tf_op jit(solution)/shard_map/ppermute | solution.py:101
  15.5 2.0 collective-permute-start.2
  18.1 0.1 copy.60
  18.3 0.1 fusion.58
  18.4 0.2 copy.57
  18.6 0.3 copy.45
  18.8 0.2 copy.41
  19.1 0.2 copy-done.5
  19.3 0.4 fusion.60
  19.6 0.1 copy.42
  19.7 0.1 copy.43
  19.9 0.3 concatenate.35
  20.2 1.1 fusion.40
  21.3 6.1 %fusion.62 = (f32[2,8,128]{2,1,0:T(8,128)S(1)}, f32[2,8,128,1152]{2,3,1,0:T(8,128)}) fusion(pred[128,1152]{0,1:T(8,128)(4,1)S(1)} %fusion.40, bf16[128,2,8,128]{3,2,1,0:T(8,128)(2,1)S(1)} %bitcast.121, bf16[64,2,128]{2,0,1:T(8,128)(2,1)S(1)} %get-tuple-element.55, bf16[64,2,128]{2,0,1:T(8,128)(2,1)S(1)} %get-tuple-element.56, ...), kind=kOutput, calls=%fused_computation.98 | convolution fusion | flops 617546880 | bytes 10706944 | tf_op jit(solution)/shard_map/sub | solution.py:47
  27.4 4.7 %fusion.20 = bf16[2,128,8,128]{3,1,2,0:T(8,128)(2,1)S(1)} fusion(f32[2,8,128,1152]{2,3,1,0:T(8,128)} %get-tuple-element.48, f32[2,8,128]{2,1,0:T(8,128)S(1)} %get-tuple-element.47, bf16[1152,2,128]{0,2,1:T(8,128)(2,1)S(1)} %concatenate.35), kind=kOutput, calls=%fused_computation.31 | convolution fusion | flops 608960512 | bytes 10559488 | tf_op jit(solution)/shard_map/qizo,oqx->zqix/dot_general | solution.py:49
  32.2 0.1 all_gather_reshape.3
  32.2 17.6 %all_gather.15 = s32[8,128,8]{1,2,0:T(8,128)S(1)} all-gather(s32[1,128,8]{1,2,0:T(8,128)S(1)} %all_gather_reshape.3), channel_id=1, replica_groups=mesh['rep'=2,'ep'=8,'tp'=2] {'ep'}, dimensions={0}, use_global_device_ids=true | all-gather | bytes 36864 | tf_op jit(solution)/shard_map/all_gather | solution.py:137
  49.8 6.6 %collective-permute-done.2 = bf16[1024,16]{0,1:T(8,128)(2,1)S(1)} collective-permute-done((bf16[1024,16]{0,1:T(8,128)(2,1)S(1)}, bf16[1024,16]{0,1:T(8,128)(2,1)S(1)}, u32[]{:S(2)}, u32[]{:S(2)}) %collective-permute-start.2) | collective-permute-done | bytes 32800 | tf_op jit(solution)/shard_map/ppermute | solution.py:101
  56.5 2.2 broadcast_select_fusion.1
  58.7 1.9 pad_maximum_fusion
  60.6 2.9 %convolution_convert_fusion = bf16[128,1024]{1,0:T(8,128)(2,1)S(1)} fusion(bf16[128,2048]{0,1:T(8,128)(2,1)S(1)} %bitcast.114, bf16[2048,1024]{1,0:T(8,128)(2,1)} %all-gather.7.cloned.1.call-done), kind=kOutput, calls=%fused_computation.36 | convolution fusion | flops 537001984 | bytes 4980736 | tf_op jit(solution)/shard_map/dot_general | solution.py:150
  63.6 1.8 collective-permute-start.4
  65.4 42.0 %all-gather.5.cloned.1.call-done = bf16[2048,1024]{1,0:T(8,128)(2,1)} async-done(((bf16[2048,128]{1,0:T(8,128)(2,1)}), bf16[2048,1024]{1,0:T(8,128)(2,1)}) %all-gather.5.cloned.1.call-update) | async-done | bytes 4194320 | tf_op jit(solution)/shard_map/all_gather | solution.py:147
  107.3 2.9 %convolution_convert_fusion.1 = bf16[128,1024]{1,0:T(8,128)(2,1)S(1)} fusion(bf16[128,2048]{0,1:T(8,128)(2,1)S(1)} %bitcast.115, bf16[2048,1024]{1,0:T(8,128)(2,1)} %all-gather.5.cloned.1.call-done), kind=kOutput, calls=%fused_computation.37 | convolution fusion | flops 537001984 | bytes 4980736 | tf_op jit(solution)/shard_map/dot_general | solution.py:150
  110.3 1.5 collective-permute-start.3
  111.9 0.1 copy.62
  112.0 6.8 %collective-permute-done.3 = bf16[128,1024]{1,0:T(8,128)(2,1)S(1)} collective-permute-done((bf16[128,1024]{1,0:T(8,128)(2,1)S(1)}, bf16[128,1024]{1,0:T(8,128)(2,1)S(1)}, u32[]{:S(2)}, u32[]{:S(2)}) %collective-permute-start.3) | collective-permute-done | bytes 262176 | tf_op jit(solution)/shard_map/ppermute | solution.py:101
  118.9 0.1 copy.61
  119.0 0.8 copy.51
  119.9 0.8 reshape.71
  120.7 0.2 fusion.35
  121.0 0.2 fusion.36
  121.1 0.8 fusion.59
  122.0 0.5 all-gather.11.cloned.1.call-update
  122.6 0.2 reduce-scatter.3.cloned.1.call-start
  122.9 0.1 fusion.61
  123.0 0.1 reshape.72
  123.1 26.4 %all-gather.9.cloned.1.call-done = bf16[512,2048]{1,0:T(8,128)(2,1)} async-done(((bf16[64,2048]{1,0:T(8,128)(2,1)}), bf16[512,2048]{1,0:T(8,128)(2,1)}) %all-gather.9.cloned.1.call-update) | async-done | bytes 2097168 | tf_op jit(solution)/shard_map/all_gather | solution.py:160
  149.5 3.4 %fusion.12 = f32[512,384]{1,0:T(8,128)S(1)} fusion(bf16[512,2048]{1,0:T(8,128)(2,1)} %all-gather.9.cloned.1.call-done, bf16[2,2048,384]{2,1,0:T(8,128)(2,1)} %pad_maximum_fusion), kind=kOutput, calls=%fused_computation.20 | convolution fusion | flops 805306368 | bytes 4456448 | tf_op jit(solution)/shard_map/dot_general | solution.py:173
  152.9 0.2 copy-done.3
  153.1 1.3 fusion.30
  154.4 1.5 collective-permute-start.5
  155.9 0.7 fusion.65
  156.6 0.1 select_reduce_fusion.3
  156.7 1.9 fusion.38
  158.6 7.1 %collective-permute-done.5 = bf16[512,384]{1,0:T(8,128)(2,1)S(1)} collective-permute-done((bf16[512,384]{1,0:T(8,128)(2,1)S(1)}, bf16[512,384]{1,0:T(8,128)(2,1)S(1)}, u32[]{:S(2)}, u32[]{:S(2)}) %collective-permute-start.5) | collective-permute-done | bytes 393248 | tf_op jit(solution)/shard_map/ppermute | solution.py:101
  165.7 2.9 %add_convert_fusion.1 = bf16[512,1024]{1,0:T(8,128)(2,1)} fusion(f32[512,1024]{1,0:T(8,128)S(1)} %fusion.38, bf16[512,384]{1,0:T(8,128)(2,1)S(1)} %collective-permute-done.5, f32[512]{0:T(512)S(1)} %get-tuple-element.24, f32[512]{0:T(512)S(1)} %get-tuple-element.23, bf16[2,3,1024,384]{3,2,1,0:T(8,128)(2,1)} %param.19, s32[]{:T(128)S(6)} %select_n.86, ...), kind=kOutput, calls=%fused_computation.11 | convolution fusion | flops 404750336 | bytes 4329480 | tf_op jit(solution)/shard_map/dot_general | solution.py:164
  168.6 10.9 %all-gather.11.cloned.1.call-done = bf16[512,2048]{1,0:T(8,128)(2,1)} async-done(((bf16[64,2048]{1,0:T(8,128)(2,1)}), bf16[512,2048]{1,0:T(8,128)(2,1)}) %all-gather.11.cloned.1.call-update) | async-done | bytes 2097168 | tf_op jit(solution)/shard_map/all_gather | solution.py:160
  179.6 0.1 reshape.73
  179.7 3.4 %fusion.10 = f32[512,384]{1,0:T(8,128)S(1)} fusion(bf16[512,2048]{1,0:T(8,128)(2,1)} %all-gather.11.cloned.1.call-done, bf16[2,2048,384]{2,1,0:T(8,128)(2,1)} %pad_maximum_fusion), kind=kOutput, calls=%fused_computation.18 | convolution fusion | flops 805306368 | bytes 4456448 | tf_op jit(solution)/shard_map/dot_general | solution.py:173
  183.2 0.2 copy-done.2
  183.4 1.3 fusion.27
  184.6 1.5 collective-permute-start.6
  186.2 0.7 fusion.66
  186.8 0.1 select_reduce_fusion.1
  186.9 1.9 fusion.37
  188.8 7.1 %collective-permute-done.6 = bf16[512,384]{1,0:T(8,128)(2,1)S(1)} collective-permute-done((bf16[512,384]{1,0:T(8,128)(2,1)S(1)}, bf16[512,384]{1,0:T(8,128)(2,1)S(1)}, u32[]{:S(2)}, u32[]{:S(2)}) %collective-permute-start.6) | collective-permute-done | bytes 393248 | tf_op jit(solution)/shard_map/ppermute | solution.py:101
  195.9 2.9 %add_convert_fusion = bf16[512,1024]{1,0:T(8,128)(2,1)} fusion(f32[512,1024]{1,0:T(8,128)S(1)} %fusion.37, bf16[512,384]{1,0:T(8,128)(2,1)S(1)} %collective-permute-done.6, f32[512]{0:T(512)S(1)} %get-tuple-element.22, f32[512]{0:T(512)S(1)} %get-tuple-element.21, bf16[2,3,1024,384]{3,2,1,0:T(8,128)(2,1)} %param.19, s32[]{:T(128)S(6)} %select_n.86, s32[]{:T(128)S(6)} %add.79), kind=kOutput, calls=%fused_computation.10 | convolution fusion | flops 404750336 | bytes 4329480 | tf_op jit(solution)/shard_map/dot_general | solution.py:164
  198.8 14.9 %reduce-scatter.3.cloned.1.call-done = bf16[64,1024]{1,0:T(8,128)(2,1)} async-done(((bf16[512,1024]{1,0:T(8,128)(2,1)}), bf16[64,1024]{1,0:T(8,128)(2,1)}) %reduce-scatter.3.cloned.1.call-update) | async-done | bytes 131088 | tf_op jit(solution)/shard_map/reduce_scatter | solution.py:190
  213.8 32.9 %reduce-scatter.5.cloned.1.call-done = bf16[64,1024]{1,0:T(8,128)(2,1)} async-done(((bf16[512,1024]{1,0:T(8,128)(2,1)}), bf16[64,1024]{1,0:T(8,128)(2,1)}) %reduce-scatter.5.cloned.1.call-update) | async-done | bytes 131088 | tf_op jit(solution)/shard_map/reduce_scatter | solution.py:190
  246.7 1.8 add_convert_fusion.3
  (49 shorter events, 0.7 us)
Async XLA Ops:
  6.5 54.1 %all-gather.7.cloned.1.call-start = ((), (), s32[]{:S(2)}) async-start(), calls=%async_computation.3 | async-start | bytes 4718592 | tf_op jit(solution)/shard_map/all_gather | solution.py:147
  8.8 6.7 %copy-start.7 = (bf16[2,64,1024]{2,1,0:T(8,128)(2,1)S(1)}, bf16[2,64,1024]{2,1,0:T(8,128)(2,1)}, u32[]{:S(2)}) copy-start(bf16[2,64,1024]{2,1,0:T(8,128)(2,1)} %param.12) | copy-start | bytes 786436
  8.8 6.7 %copy-start.8 = (bf16[1024,16]{0,1:T(8,128)(2,1)S(1)}, bf16[1024,16]{0,1:T(8,128)(2,1)}, u32[]{:S(2)}) copy-start(bf16[1024,16]{0,1:T(8,128)(2,1)} %param.18) | copy-start | bytes 98308
  8.8 9.3 %copy-start.6 = (bf16[2,64,2048]{2,1,0:T(8,128)(2,1)S(1)}, bf16[2,64,2048]{2,1,0:T(8,128)(2,1)}, u32[]{:S(2)}) copy-start(bf16[2,64,2048]{2,1,0:T(8,128)(2,1)} %param.13) | copy-start | bytes 1572868
  8.8 98.5 %all-gather.5.cloned.1.call-start = ((), (), s32[]{:S(2)}) async-start(), calls=%async_computation.2 | async-start | bytes 4718592 | tf_op jit(solution)/shard_map/all_gather | solution.py:147
  9.6 139.9 %all-gather.9.cloned.1.call-start = ((), (), s32[]{:S(2)}) async-start(), calls=%async_computation.4 | async-start | bytes 2359296 | tf_op jit(solution)/shard_map/all_gather | solution.py:160
  9.6 8.6 %copy-start.4 = (bf16[1,2,1024,256]{3,2,1,0:T(8,128)(2,1)S(1)}, bf16[1,2,1024,256]{3,2,1,0:T(8,128)(2,1)}, u32[]{:S(2)}) copy-start(bf16[1,2,1024,256]{3,2,1,0:T(8,128)(2,1)} %param.15) | copy-start | bytes 3145732
  12.5 44.0 %collective-permute-start = (bf16[2,1024,384]{2,1,0:T(8,128)(2,1)}, bf16[2,1024,384]{2,1,0:T(8,128)(2,1)}, u32[]{:S(2)}, u32[]{:S(2)}) collective-permute-start(bf16[2,1024,384]{2,1,0:T(8,128)(2,1)} %dynamic-slice_bitcast_fusion), channel_id=1, source_target_pairs={{0,1},{1,0},{2,3},{3,2},{4,5},{5,4},{6,7},{7,6},{8,9},{9,8},{10,11... | collective-permute-start | bytes 4718600 | tf_op jit(solution)/shard_map/ppermute | solution.py:101
  15.4 40.9 %collective-permute-start.1 = (bf16[128,1024]{1,0:T(8,128)(2,1)S(1)}, bf16[128,1024]{1,0:T(8,128)(2,1)S(1)}, u32[]{:S(2)}, u32[]{:S(2)}) collective-permute-start(bf16[128,1024]{1,0:T(8,128)(2,1)S(1)} %bitcast.124), channel_id=1, source_target_pairs={{0,1},{1,0},{2,3},{3,2},{4,5},{5,4},{6,7},{7,6},{8,9},{9,8},{10,11... | collective-permute-start | bytes 786440 | tf_op jit(solution)/shard_map/ppermute | solution.py:101
  15.5 40.9 %collective-permute-start.2 = (bf16[1024,16]{0,1:T(8,128)(2,1)S(1)}, bf16[1024,16]{0,1:T(8,128)(2,1)S(1)}, u32[]{:S(2)}, u32[]{:S(2)}) collective-permute-start(bf16[1024,16]{0,1:T(8,128)(2,1)S(1)} %copy-done.8), channel_id=1, source_target_pairs={{0,1},{1,0},{2,3},{3,2},{4,5},{5,4},{6,7},{7,6},{8,9},{9,8},{10,11... | collective-permute-start | bytes 98312 | tf_op jit(solution)/shard_map/ppermute | solution.py:101
  18.3 0.9 copy-start.5
  27.4 4.7 %copy-start.9 = (s32[2,64,8]{1,2,0:T(8,128)S(1)}, s32[2,64,8]{1,2,0:T(8,128)}, u32[]{:S(2)}) copy-start(s32[2,64,8]{1,2,0:T(8,128)} %param.20) | copy-start | bytes 12292
  63.6 48.2 %collective-permute-start.4 = (bf16[128,1024]{1,0:T(8,128)(2,1)S(1)}, bf16[128,1024]{1,0:T(8,128)(2,1)S(1)}, u32[]{:S(2)}, u32[]{:S(2)}) collective-permute-start(bf16[128,1024]{1,0:T(8,128)(2,1)S(1)} %convolution_convert_fusion), channel_id=1, source_target_pairs={{0,1},{1,0},{2,3},{3,2},{4,5},{5,4},{6,7},{7,6},{8,9},{9,8},{10,11... | collective-permute-start | bytes 786440 | tf_op jit(solution)/shard_map/ppermute | solution.py:101
  110.3 8.5 %collective-permute-start.3 = (bf16[128,1024]{1,0:T(8,128)(2,1)S(1)}, bf16[128,1024]{1,0:T(8,128)(2,1)S(1)}, u32[]{:S(2)}, u32[]{:S(2)}) collective-permute-start(bf16[128,1024]{1,0:T(8,128)(2,1)S(1)} %convolution_convert_fusion.1), channel_id=1, source_target_pairs={{0,1},{1,0},{2,3},{3,2},{4,5},{5,4},{6,7},{7,6},{8,9},{9,8},{10,11... | collective-permute-start | bytes 786440 | tf_op jit(solution)/shard_map/ppermute | solution.py:101
  120.7 2.1 copy-start.10
  122.0 57.5 %all-gather.11.cloned.1.call-start = ((), (), s32[]{:S(2)}) async-start(), calls=%async_computation.5 | async-start | bytes 2359296 | tf_op jit(solution)/shard_map/all_gather | solution.py:160
  122.6 91.2 %reduce-scatter.3.cloned.1.call-start = ((), (), s32[]{:S(2)}) async-start(), calls=%async_computation.6 | async-start | bytes 1179648 | tf_op jit(solution)/shard_map/reduce_scatter | solution.py:190
  149.5 3.4 %copy-start = (bf16[2,2048,384]{2,1,0:T(8,128)(2,1)S(1)}, bf16[2,2048,384]{2,1,0:T(8,128)(2,1)}, u32[]{:S(2)}) copy-start(bf16[2,2048,384]{2,1,0:T(8,128)(2,1)} %pad_maximum_fusion) | copy-start | bytes 9437188
  149.5 3.6 %copy-start.3 = (bf16[512,2048]{1,0:T(8,128)(2,1)S(1)}, bf16[512,2048]{1,0:T(8,128)(2,1)}, u32[]{:S(2)}) copy-start(bf16[512,2048]{1,0:T(8,128)(2,1)} %all-gather.9.cloned.1.call-done) | copy-start | bytes 6291460
  154.4 11.3 %collective-permute-start.5 = (bf16[512,384]{1,0:T(8,128)(2,1)S(1)}, bf16[512,384]{1,0:T(8,128)(2,1)S(1)}, u32[]{:S(2)}, u32[]{:S(2)}) collective-permute-start(bf16[512,384]{1,0:T(8,128)(2,1)S(1)} %fusion.30), channel_id=1, source_target_pairs={{0,1},{1,0},{2,3},{3,2},{4,5},{5,4},{6,7},{7,6},{8,9},{9,8},{10,11... | collective-permute-start | bytes 1179656 | tf_op jit(solution)/shard_map/ppermute | solution.py:101
  179.5 67.1 %reduce-scatter.5.cloned.1.call-start = ((), (), s32[]{:S(2)}) async-start(), calls=%async_computation.7 | async-start | bytes 1179648 | tf_op jit(solution)/shard_map/reduce_scatter | solution.py:190
  179.7 3.5 %copy-start.1 = (bf16[2,2048,384]{2,1,0:T(8,128)(2,1)S(1)}, bf16[2,2048,384]{2,1,0:T(8,128)(2,1)}, u32[]{:S(2)}) copy-start(bf16[2,2048,384]{2,1,0:T(8,128)(2,1)} %pad_maximum_fusion) | copy-start | bytes 9437188
  179.7 3.6 %copy-start.2 = (bf16[512,2048]{1,0:T(8,128)(2,1)S(1)}, bf16[512,2048]{1,0:T(8,128)(2,1)}, u32[]{:S(2)}) copy-start(bf16[512,2048]{1,0:T(8,128)(2,1)} %all-gather.11.cloned.1.call-done) | copy-start | bytes 6291460
  184.6 11.3 %collective-permute-start.6 = (bf16[512,384]{1,0:T(8,128)(2,1)S(1)}, bf16[512,384]{1,0:T(8,128)(2,1)S(1)}, u32[]{:S(2)}, u32[]{:S(2)}) collective-permute-start(bf16[512,384]{1,0:T(8,128)(2,1)S(1)} %fusion.27), channel_id=1, source_target_pairs={{0,1},{1,0},{2,3},{3,2},{4,5},{5,4},{6,7},{7,6},{8,9},{9,8},{10,11... | collective-permute-start | bytes 1179656 | tf_op jit(solution)/shard_map/ppermute | solution.py:101
Sparse Core Ops, SparseCore 0:
  8.9 50.7 all-gather.6
  61.3 45.9 all-gather.4
  122.1 27.3 all-gather.8
  150.9 28.5 all-gather.10
  181.6 32.0 reduce-scatter.2
  215.9 30.7 reduce-scatter.4

commit v4 on v2

--- a/solution.py
+++ b/solution.py
@@ -117,9 +117,9 @@
     tokens_dev, width = attention.shape[0], hidden_states.shape[1]
     experts = slot_table.shape[0]
     local_slots = weights.shape[0]
-    groups = lax.axis_size("ep")
     mine = lax.axis_index("tp")
     theirs = 1 - mine
+    projection = lax.all_gather(out_weight, "ep", axis=1, tiled=True)
     own_gate_up = pick(weights, mine)[:2]
     sent_gate_up = swap(pick(weights, theirs)[:2])
     first = mine == 0
@@ -132,10 +132,15 @@
     )
     hidden_full = both_halves(hidden_states, 1)
     router_full = both_halves(router_weight, 0)
+    routed_all = lax.all_gather(routed, "ep", axis=0, tiled=True)
+    attention, gate_up_weight, hidden_full, router_full, routed_all = lax.optimization_barrier(
+        (attention, gate_up_weight, hidden_full, router_full, routed_all)
+    )
+    slots = jnp.arange(experts, dtype=jnp.int32)
+    marks = (routed_all[:, :, None] == slots).any(1)
+    base_slot = lax.axis_index("ep") * local_slots
     head_terms = jnp.dot(
-        attention,
-        lax.all_gather(out_weight, "ep", axis=1, tiled=True),
-        preferred_element_type=jnp.float32,
+        attention, projection, preferred_element_type=jnp.float32
     ).astype(jnp.bfloat16)
     attn_out = head_terms.astype(jnp.float32) + swap(head_terms).astype(jnp.float32)
     residual = (hidden_full.astype(jnp.float32) + attn_out).astype(jnp.bfloat16)
@@ -143,35 +148,26 @@
     squares = jnp.sum(wide * wide, 1)
     normed = (wide * lax.rsqrt(squares / D + 1e-06)[:, None]).astype(jnp.bfloat16)
     rows = lax.all_gather(normed, "ep", axis=0, tiled=True)
-    logits = jnp.dot(normed, router_full, preferred_element_type=jnp.float32)
-    slot_of = lookup(slot_table, routed)
-    marks = routed[:, :, None] == jnp.arange(experts, dtype=jnp.int32)
-    raised = jnp.where(marks.any(1), jnp.exp(logits), 0.0)
-    combine = raised / jnp.sum(raised, 1, keepdims=True)
-    picked = jnp.sum(jnp.where(marks, combine[:, None, :], 0.0), 2)
-    by_slot = jnp.sum(
-        jnp.where(
-            slot_of[:, :, None] == jnp.arange(experts, dtype=jnp.int32), picked[:, :, None], 0.0
-        ),
-        1,
-    )
-    shares = lax.all_gather(by_slot, "ep", axis=0, tiled=True)
-    local = jnp.arange(experts, dtype=jnp.int32)[None, :] - lax.axis_index("ep") * local_slots
-    own_share = jnp.sum(jnp.where(local == mine, shares, 0.0), 1, keepdims=True)
-    their_share = jnp.sum(jnp.where(local == theirs, shares, 0.0), 1, keepdims=True)
+
+    def down(value, slot):
+        return lax.dot_general(
+            value, slot, (((1,), (1,)), ((), ())), preferred_element_type=jnp.float32
+        )
+
+    own_down = pick(weights, mine)[2]
+    their_down = pick(weights, theirs)[2]
     gate = jnp.dot(rows, gate_up_weight[0], preferred_element_type=jnp.float32)
     up = jnp.dot(rows, gate_up_weight[1], preferred_element_type=jnp.float32)
     hidden = (jax.nn.silu(gate) * up).astype(jnp.bfloat16)
     their_hidden = swap(hidden)
-
-    def down(value, slot):
-        return lax.dot_general(
-            value, slot, (((1,), (1,)), ((), ())), preferred_element_type=jnp.float32
-        )
-
-    total = own_share * down(hidden, pick(weights, mine)[2]) + their_share * down(
-        their_hidden, pick(weights, theirs)[2]
-    )
+    logits = jnp.dot(rows, router_full, preferred_element_type=jnp.float32)
+    raised = jnp.where(marks, jnp.exp(logits), 0.0)
+    combine = raised / jnp.sum(raised, 1, keepdims=True)
+    own_share = jnp.sum(jnp.where(slot_table == base_slot + mine, combine, 0.0), 1, keepdims=True)
+    their_share = jnp.sum(
+        jnp.where(slot_table == base_slot + theirs, combine, 0.0), 1, keepdims=True
+    )
+    total = own_share * down(hidden, own_down) + their_share * down(their_hidden, their_down)
     mixed = lax.psum_scatter(
         total.astype(jnp.bfloat16), "ep", scatter_dimension=0, tiled=True
     ).astype(jnp.float32)

time: 240 us -> 235 us (0.979)
  waiting for transfers between devices: 163 us -> 145 us
  blocking collectives: 14.1 us -> 18.6 us
  matrix products: 30.1 us -> 32.8 us
  starting transfers between devices: 5.8 us -> 8.37 us
    all_gather x1, waiting for transfers between devices: 3.43 us -> 44.9 us  [gathered_layer(): rows = lax.all_gather(normed, 'ep', axis=0, tiled=True)]
    all_gather x1, waiting for transfers between devices: 70.5 us -> 35.5 us  [gathered_layer(): projection = lax.all_gather(out_weight, 'ep', axis=1, tiled=True)]
    ppermute x5, waiting for transfers between devices: 53.3 us -> 28.8 us  [swap(): return lax.ppermute(value, 'tp', [(0, 1), (1, 0)])]
    all_gather x1, blocking collectives: 14.1 us -> 18.6 us  [gathered_layer(): routed_all = lax.all_gather(routed, 'ep', axis=0, tiled=True)]
    sub x1, matrix products: 6.12 us -> 8.63 us  [attend_local(): attention_scores - largest]
  transfers between devices with their start and end apart: 8 -> 8, of which waited for: 6 -> 6; matrix products, arithmetic and copies ran while one was open for 10% -> 12% of each run, Pallas kernels for 0% -> 0%
where the time goes in v4:
time: 235 us; the launch traced here: 234 us
  waiting for transfers between devices  145 us (62%)
  matrix products  32.8 us (14%)
  blocking collectives  18.6 us (8%)
  between operations  14 us (6%)
  other arithmetic  10.3 us (4%)
  starting transfers between devices  8.37 us (4%)
  local copies, waits for them, and re-layouts  5.1 us (2%)
    all_gather x1, waiting for transfers between devices, gathered_layer(): rows = lax.all_gather(normed, 'ep', axis=0, tiled=True)  44.9 us
    all_gather x1, waiting for transfers between devices, gathered_layer(): projection = lax.all_gather(out_weight, 'ep', axis=1, tiled=True)  35.5 us
    reduce_scatter x1, waiting for transfers between devices, gathered_layer(): lax.psum_scatter(total.astype(jnp.bfloat16), 'ep', scatter_dimension=0, t...  35 us
    ppermute x5, waiting for transfers between devices, swap(): return lax.ppermute(value, 'tp', [(0, 1), (1, 0)])  28.8 us
    all_gather x1, blocking collectives, gathered_layer(): routed_all = lax.all_gather(routed, 'ep', axis=0, tiled=True)  18.6 us
    sub x1, matrix products, attend_local(): attention_scores - largest  8.63 us
    ppermute x5, starting transfers between devices, swap(): return lax.ppermute(value, 'tp', [(0, 1), (1, 0)])  8.1 us
    dot_general x2, matrix products, down(): lax.dot_general(value, slot, (((1,), (1,)), ((), ())), preferred_element_...  6.2 us
  transfers between devices with their start and end apart: 8, of which 6 were waited for; matrix products, arithmetic and copies ran while one was open for 12% of the time, Pallas kernels for 0%

profile of v4, /device:TPU:0, one launch (start us, length us, event | category | flops | bytes accessed | tf_op | source)
XLA Modules:
  0.0 234.2 jit_solution(13072930124949817343)
XLA Ops:
  6.5 0.0 copy-start.5
  6.5 0.0 copy-start.4
  6.5 0.0 all-gather.3.cloned.1.call-start
  6.5 0.7 all-gather.3.cloned.1.call-update
  7.3 0.0 all-gather.5.cloned.1.call-start
  7.3 0.0 copy-start.2
  7.3 0.0 copy-start.3
  7.3 1.7 dynamic-slice_bitcast_fusion
  9.0 3.0 %collective-permute-start = (bf16[2,1024,384]{2,1,0:T(8,128)(2,1)S(1)}, bf16[2,1024,384]{2,1,0:T(8,128)(2,1)}, u32[]{:S(2)}, u32[]{:S(2)}) collective-permute-start(bf16[2,1024,384]{2,1,0:T(8,128)(2,1)S(1)} %dynamic-slice_bitcast_fusion), channel_id=1, source_target_pairs={{0,1},{1,0},{2,3},{3,2},{4,5},{5,4},{6,7},{7,6},{8,9},{9,8},{10,11... | collective-permute-start | bytes 4718600 | tf_op jit(solution)/shard_map/ppermute | solution.py:99
  12.0 0.0 copy-done.5
  12.0 0.1 collective-permute-start.1
  12.1 1.9 collective-permute-start.2
  14.7 0.0 copy-done.4
  14.7 0.9 copy.43
  15.6 0.0 copy-done.2
  15.7 0.1 fusion.37
  15.7 0.2 copy.40
  15.9 1.0 copy.31
  16.9 0.2 copy.27
  17.1 0.0 copy-done.3
  17.1 0.4 fusion.38
  17.5 0.1 copy.28
  17.6 0.1 copy.29
  17.8 0.3 concatenate.32
  18.1 1.1 fusion.22
  19.2 8.6 %fusion.39 = (f32[2,8,128]{2,1,0:T(8,128)S(1)}, f32[2,8,128,1152]{2,3,1,0:T(8,128)}) fusion(pred[128,1152]{0,1:T(8,128)(4,1)S(1)} %fusion.22, bf16[128,2,8,128]{3,2,1,0:T(8,128)(2,1)} %bitcast.84, bf16[64,2,128]{2,0,1:T(8,128)(2,1)S(1)} %get-tuple-element.41, bf16[64,2,128]{2,0,1:T(8,128)(2,1)S(1)} %get-tuple-element.42, bf16[1024,2,128]{2,0,1:T(8,128)(2,1)} %copy.31), kind=kOutput, calls=%fused_computation.73 | convolution fusion | flops 617546880 | bytes 10706944 | tf_op jit(solution)/shard_map/sub | solution.py:45
  27.8 0.0 copy-start.6
  27.8 4.6 %fusion.16 = bf16[2,128,8,128]{3,1,2,0:T(8,128)(2,1)S(1)} fusion(f32[2,8,128,1152]{2,3,1,0:T(8,128)} %get-tuple-element.36, f32[2,8,128]{2,1,0:T(8,128)S(1)} %get-tuple-element.35, bf16[1152,2,128]{0,2,1:T(8,128)(2,1)S(1)} %concatenate.32), kind=kOutput, calls=%fused_computation.26 | convolution fusion | flops 608960512 | bytes 10559488 | tf_op jit(solution)/shard_map/qizo,oqx->zqix/dot_general | solution.py:47
  32.4 0.0 copy-done.6
  32.4 0.1 reshape.62
  32.5 18.6 %all_gather.9 = s32[1024,8]{0,1:T(8,128)S(1)} all-gather(s32[128,8]{0,1:T(8,128)S(1)} %reshape.62), channel_id=1, replica_groups=mesh['rep'=2,'ep'=8,'tp'=2] {'ep'}, dimensions={0}, use_global_device_ids=true | all-gather | bytes 36864 | tf_op jit(solution)/shard_map/all_gather | solution.py:135
  51.1 1.8 collective-permute-done.2
  52.9 0.8 broadcast_select_fusion.5
  53.6 0.0 collective-permute-done.1
  53.7 1.0 broadcast_select_fusion.3
  54.7 0.0 collective-permute-done
  54.7 2.2 broadcast_select_fusion.1
  56.9 2.0 pad_maximum_fusion
  58.9 0.0 copy-start.7
  58.9 35.5 %all-gather.3.cloned.1.call-done = bf16[2048,2048]{1,0:T(8,128)(2,1)} async-done(((bf16[2048,256]{1,0:T(8,128)(2,1)}), bf16[2048,2048]{1,0:T(8,128)(2,1)}) %all-gather.3.cloned.1.call-update) | async-done | bytes 8388624 | tf_op jit(solution)/shard_map/all_gather | solution.py:122
  94.4 4.7 %convolution_convert_fusion = bf16[128,2048]{1,0:T(8,128)(2,1)S(1)} fusion(bf16[128,2048]{0,1:T(8,128)(2,1)S(1)} %bitcast.82, bf16[2048,2048]{1,0:T(8,128)(2,1)} %all-gather.3.cloned.1.call-done), kind=kOutput, calls=%fused_computation.11 | convolution fusion | flops 1074003968 | bytes 9437184 | tf_op jit(solution)/shard_map/dot_general | solution.py:142
  99.1 1.5 collective-permute-start.3
  100.6 12.6 %collective-permute-done.3 = bf16[128,2048]{1,0:T(8,128)(2,1)S(1)} collective-permute-done((bf16[128,2048]{1,0:T(8,128)(2,1)S(1)}, bf16[128,2048]{1,0:T(8,128)(2,1)S(1)}, u32[]{:S(2)}, u32[]{:S(2)}) %collective-permute-start.3) | collective-permute-done | bytes 524320 | tf_op jit(solution)/shard_map/ppermute | solution.py:99
  113.2 0.4 fusion.18
  113.6 0.9 fusion.19
  114.5 0.0 all-gather.5.cloned.1.call-update
  114.6 0.2 reduce-scatter.2.cloned.1.call-start
  114.8 0.0 copy-done.7
  114.8 0.1 fusion.23
  114.9 44.9 %all-gather.5.cloned.1.call-done = bf16[1024,2048]{1,0:T(8,128)(2,1)} async-done(((bf16[128,2048]{1,0:T(8,128)(2,1)}), bf16[1024,2048]{1,0:T(8,128)(2,1)}) %all-gather.5.cloned.1.call-update) | async-done | bytes 4194320 | tf_op jit(solution)/shard_map/all_gather | solution.py:150
  159.8 0.0 copy-start.1
  159.8 5.1 %fusion.8 = f32[1024,384]{1,0:T(8,128)S(1)} fusion(bf16[1024,2048]{1,0:T(8,128)(2,1)} %all-gather.5.cloned.1.call-done, bf16[2,2048,384]{2,1,0:T(8,128)(2,1)} %pad_maximum_fusion), kind=kOutput, calls=%fused_computation.16 | convolution fusion | flops 1610612736 | bytes 7340032 | tf_op jit(solution)/shard_map/dot_general | solution.py:159
  164.9 0.0 copy-done
  164.9 0.0 copy-done.1
  164.9 2.4 %multiply_convert_fusion = bf16[1024,384]{1,0:T(8,128)(2,1)S(1)} fusion(f32[1024,384]{1,0:T(8,128)S(1)} %fusion.8, bf16[1024,2048]{1,0:T(8,128)(2,1)S(1)} %copy-done, bf16[2,2048,384]{2,1,0:T(8,128)(2,1)S(1)} %copy-done.1), kind=kOutput, calls=%fused_computation.18 | convolution fusion | flops 1612972032 | bytes 8126464 | tf_op jit(solution)/shard_map/dot_general | solution.py:160
  167.4 1.5 collective-permute-start.4
  168.9 1.2 fusion.42
  170.1 0.1 select_reduce_fusion.1
  170.2 2.4 %fusion.20 = f32[1024,1024]{1,0:T(8,128)S(1)} fusion(bf16[1024,384]{1,0:T(8,128)(2,1)S(1)} %multiply_convert_fusion, bf16[2,3,1024,384]{3,2,1,0:T(8,128)(2,1)} %param.19, s32[]{:T(128)S(6)} %select_n.76, s32[]{:T(128)S(6)} %add.63), kind=kOutput, calls=%fused_computation.34 | convolution fusion | flops 805306368 | bytes 5767176 | tf_op jit(solution)/shard_map/dot_general | solution.py:153
  172.6 14.5 %collective-permute-done.4 = bf16[1024,384]{1,0:T(8,128)(2,1)S(1)} collective-permute-done((bf16[1024,384]{1,0:T(8,128)(2,1)S(1)}, bf16[1024,384]{1,0:T(8,128)(2,1)S(1)}, u32[]{:S(2)}, u32[]{:S(2)}) %collective-permute-start.4) | collective-permute-done | bytes 786464 | tf_op jit(solution)/shard_map/ppermute | solution.py:99
  187.1 3.8 %add_convert_fusion = bf16[1024,1024]{1,0:T(8,128)(2,1)} fusion(f32[1024,1024]{1,0:T(8,128)S(1)} %fusion.20, bf16[1024,384]{1,0:T(8,128)(2,1)S(1)} %collective-permute-done.4, f32[1024]{0:T(1024)S(1)} %get-tuple-element.18, f32[1024]{0:T(1024)S(1)} %get-tuple-element.17, bf16[2,3,1024,384]{3,2,1,0:T(8,128)(2,1)} %param.19, s32[]{:T(128)S(6)} %select_n.77, ...), kind=kOutput, calls=%fused_computation.9 | convolution fusion | flops 809500672 | bytes 7872520 | tf_op jit(solution)/shard_map/dot_general | solution.py:153
  190.9 0.0 reduce-scatter.2.cloned.1.call-update
  190.9 35.0 %reduce-scatter.2.cloned.1.call-done = bf16[128,1024]{1,0:T(8,128)(2,1)} async-done(((bf16[1024,1024]{1,0:T(8,128)(2,1)}), bf16[128,1024]{1,0:T(8,128)(2,1)}) %reduce-scatter.2.cloned.1.call-update) | async-done | bytes 262160 | tf_op jit(solution)/shard_map/reduce_scatter | solution.py:171
  225.9 1.8 add_convert_fusion.2
  (9 shorter events, 0.1 us)
Async XLA Ops:
  6.5 5.5 %copy-start.5 = (bf16[2,64,1024]{2,1,0:T(8,128)(2,1)S(1)}, bf16[2,64,1024]{2,1,0:T(8,128)(2,1)}, u32[]{:S(2)}) copy-start(bf16[2,64,1024]{2,1,0:T(8,128)(2,1)} %param.12) | copy-start | bytes 786436
  6.5 8.2 %copy-start.4 = (bf16[2,64,2048]{2,1,0:T(8,128)(2,1)S(1)}, bf16[2,64,2048]{2,1,0:T(8,128)(2,1)}, u32[]{:S(2)}) copy-start(bf16[2,64,2048]{2,1,0:T(8,128)(2,1)} %param.13) | copy-start | bytes 1572868
  6.5 87.9 %all-gather.3.cloned.1.call-start = ((), (), s32[]{:S(2)}) async-start(), calls=%async_computation.1 | async-start | bytes 9437184 | tf_op jit(solution)/shard_map/all_gather | solution.py:122
  7.3 152.5 %all-gather.5.cloned.1.call-start = ((), (), s32[]{:S(2)}) async-start(), calls=%async_computation.2 | async-start | bytes 4718592 | tf_op jit(solution)/shard_map/all_gather | solution.py:150
  7.3 8.3 %copy-start.2 = (bf16[1,2,1024,256]{3,2,1,0:T(8,128)(2,1)S(1)}, bf16[1,2,1024,256]{3,2,1,0:T(8,128)(2,1)}, u32[]{:S(2)}) copy-start(bf16[1,2,1024,256]{3,2,1,0:T(8,128)(2,1)} %param.15) | copy-start | bytes 3145732
  7.3 9.8 %copy-start.3 = (bf16[2,64,2,256]{3,2,1,0:T(2,128)(2,1)S(1)}, bf16[2,64,2,256]{3,2,1,0:T(2,128)(2,1)}, u32[]{:S(2)}) copy-start(bf16[2,64,2,256]{3,2,1,0:T(2,128)(2,1)} %param.14) | copy-start | bytes 393220
  9.0 45.7 %collective-permute-start = (bf16[2,1024,384]{2,1,0:T(8,128)(2,1)S(1)}, bf16[2,1024,384]{2,1,0:T(8,128)(2,1)}, u32[]{:S(2)}, u32[]{:S(2)}) collective-permute-start(bf16[2,1024,384]{2,1,0:T(8,128)(2,1)S(1)} %dynamic-slice_bitcast_fusion), channel_id=1, source_target_pairs={{0,1},{1,0},{2,3},{3,2},{4,5},{5,4},{6,7},{7,6},{8,9},{9,8},{10,11... | collective-permute-start | bytes 4718600 | tf_op jit(solution)/shard_map/ppermute | solution.py:99
  12.0 41.6 %collective-permute-start.1 = (bf16[128,1024]{1,0:T(8,128)(2,1)S(1)}, bf16[128,1024]{1,0:T(8,128)(2,1)}, u32[]{:S(2)}, u32[]{:S(2)}) collective-permute-start(bf16[128,1024]{1,0:T(8,128)(2,1)S(1)} %bitcast.87), channel_id=1, source_target_pairs={{0,1},{1,0},{2,3},{3,2},{4,5},{5,4},{6,7},{7,6},{8,9},{9,8},{10,11... | collective-permute-start | bytes 786440 | tf_op jit(solution)/shard_map/ppermute | solution.py:99
  12.1 40.7 %collective-permute-start.2 = (bf16[1024,16]{0,1:T(8,128)(2,1)}, bf16[1024,16]{0,1:T(8,128)(2,1)}, u32[]{:S(2)}, u32[]{:S(2)}) collective-permute-start(bf16[1024,16]{0,1:T(8,128)(2,1)} %param.18), channel_id=1, source_target_pairs={{0,1},{1,0},{2,3},{3,2},{4,5},{5,4},{6,7},{7,6},{8,9},{9,8},{10,11... | collective-permute-start | bytes 98312 | tf_op jit(solution)/shard_map/ppermute | solution.py:99
  27.8 4.6 %copy-start.6 = (s32[2,64,8]{1,2,0:T(8,128)S(1)}, s32[2,64,8]{1,2,0:T(8,128)}, u32[]{:S(2)}) copy-start(s32[2,64,8]{1,2,0:T(8,128)} %param.20) | copy-start | bytes 12292
  58.9 55.9 %copy-start.7 = (s32[16]{0:T(128)S(1)}, s32[16]{0:T(128)}, u32[]{:S(2)}) copy-start(s32[16]{0:T(128)} %param.21) | copy-start | bytes 196
  99.1 14.1 %collective-permute-start.3 = (bf16[128,2048]{1,0:T(8,128)(2,1)S(1)}, bf16[128,2048]{1,0:T(8,128)(2,1)S(1)}, u32[]{:S(2)}, u32[]{:S(2)}) collective-permute-start(bf16[128,2048]{1,0:T(8,128)(2,1)S(1)} %convolution_convert_fusion), channel_id=1, source_target_pairs={{0,1},{1,0},{2,3},{3,2},{4,5},{5,4},{6,7},{7,6},{8,9},{9,8},{10,11... | collective-permute-start | bytes 1572872 | tf_op jit(solution)/shard_map/ppermute | solution.py:99
  114.6 111.3 %reduce-scatter.2.cloned.1.call-start = ((), (), s32[]{:S(2)}) async-start(), calls=%async_computation.3 | async-start | bytes 2359296 | tf_op jit(solution)/shard_map/reduce_scatter | solution.py:171
  159.8 5.1 %copy-start = (bf16[1024,2048]{1,0:T(8,128)(2,1)S(1)}, bf16[1024,2048]{1,0:T(8,128)(2,1)}, u32[]{:S(2)}) copy-start(bf16[1024,2048]{1,0:T(8,128)(2,1)} %all-gather.5.cloned.1.call-done) | copy-start | bytes 12582916
  159.8 5.2 %copy-start.1 = (bf16[2,2048,384]{2,1,0:T(8,128)(2,1)S(1)}, bf16[2,2048,384]{2,1,0:T(8,128)(2,1)}, u32[]{:S(2)}) copy-start(bf16[2,2048,384]{2,1,0:T(8,128)(2,1)} %pad_maximum_fusion) | copy-start | bytes 9437188
  167.4 19.7 %collective-permute-start.4 = (bf16[1024,384]{1,0:T(8,128)(2,1)S(1)}, bf16[1024,384]{1,0:T(8,128)(2,1)S(1)}, u32[]{:S(2)}, u32[]{:S(2)}) collective-permute-start(bf16[1024,384]{1,0:T(8,128)(2,1)S(1)} %multiply_convert_fusion), channel_id=1, source_target_pairs={{0,1},{1,0},{2,3},{3,2},{4,5},{5,4},{6,7},{7,6},{8,9},{9,8},{10,11... | collective-permute-start | bytes 2359304 | tf_op jit(solution)/shard_map/ppermute | solution.py:99
Sparse Core Ops, SparseCore 0:
  8.9 85.4 all-gather.2
  114.7 45.0 all-gather.4
  191.0 34.8 reduce-scatter.1

commit v5 on v4

--- a/solution.py
+++ b/solution.py
@@ -119,7 +119,8 @@
     local_slots = weights.shape[0]
     mine = lax.axis_index("tp")
     theirs = 1 - mine
-    projection = lax.all_gather(out_weight, "ep", axis=1, tiled=True)
+    groups = lax.axis_size("ep")
+    attention_all = lax.all_gather(attention, "ep", axis=0, tiled=True)
     own_gate_up = pick(weights, mine)[:2]
     sent_gate_up = swap(pick(weights, theirs)[:2])
     first = mine == 0
@@ -133,15 +134,19 @@
     hidden_full = both_halves(hidden_states, 1)
     router_full = both_halves(router_weight, 0)
     routed_all = lax.all_gather(routed, "ep", axis=0, tiled=True)
-    attention, gate_up_weight, hidden_full, router_full, routed_all = lax.optimization_barrier(
-        (attention, gate_up_weight, hidden_full, router_full, routed_all)
+    out_weight, gate_up_weight, hidden_full, router_full, routed_all = lax.optimization_barrier(
+        (out_weight, gate_up_weight, hidden_full, router_full, routed_all)
     )
     slots = jnp.arange(experts, dtype=jnp.int32)
     marks = (routed_all[:, :, None] == slots).any(1)
     base_slot = lax.axis_index("ep") * local_slots
-    head_terms = jnp.dot(
-        attention, projection, preferred_element_type=jnp.float32
+    column_terms = jnp.dot(
+        attention_all, out_weight, preferred_element_type=jnp.float32
     ).astype(jnp.bfloat16)
+    head_terms = lax.all_to_all(
+        column_terms.reshape(groups, tokens_dev, -1), "ep", split_axis=0, concat_axis=0, tiled=True
+    )
+    head_terms = head_terms.transpose(1, 0, 2).reshape(tokens_dev, 2 * width)
     attn_out = head_terms.astype(jnp.float32) + swap(head_terms).astype(jnp.float32)
     residual = (hidden_full.astype(jnp.float32) + attn_out).astype(jnp.bfloat16)
     wide = residual.astype(jnp.float32)

time: 235 us -> 239 us (1.017)
  blocking collectives: 18.6 us -> 36.1 us
  waiting for transfers between devices: 145 us -> 130 us
  local copies, waits for them, and re-layouts: 5.1 us -> 8.63 us
    all_gather x1, waiting for transfers between devices: 35.5 us -> 0.01 us  [gathered_layer(): attention_all = lax.all_gather(attention, 'ep', axis=0, tiled=True)]
    ppermute x5, waiting for transfers between devices: 28.8 us -> 49.2 us  [swap(): return lax.ppermute(value, 'tp', [(0, 1), (1, 0)])]
    all_to_all x0 -> x1, blocking collectives: none -> 20.3 us  [gathered_layer(): lax.all_to_all(column_terms.reshape(groups, tokens_dev, -1), 'ep', split_...]
    all_gather x1, blocking collectives: 18.6 us -> 15.9 us  [gathered_layer(): routed_all = lax.all_gather(routed, 'ep', axis=0, tiled=True)]
  transfers between devices with their start and end apart: 8 -> 8, of which waited for: 6 -> 6; matrix products, arithmetic and copies ran while one was open for 12% -> 5% of each run, Pallas kernels for 0% -> 0%
where the time goes in v5:
time: 239 us; the launch traced here: 238 us
  waiting for transfers between devices  130 us (54%)
  blocking collectives  36.1 us (15%)
  matrix products  32.2 us (13%)
  between operations  14.1 us (6%)
  local copies, waits for them, and re-layouts  8.63 us (4%)
  other arithmetic  8.62 us (4%)
  starting transfers between devices  8.35 us (3%)
    ppermute x5, waiting for transfers between devices, swap(): return lax.ppermute(value, 'tp', [(0, 1), (1, 0)])  49.2 us
    all_gather x1, waiting for transfers between devices, gathered_layer(): rows = lax.all_gather(normed, 'ep', axis=0, tiled=True)  46.2 us
    reduce_scatter x1, waiting for transfers between devices, gathered_layer(): lax.psum_scatter(total.astype(jnp.bfloat16), 'ep', scatter_dimension=0, t...  35 us
    all_to_all x1, blocking collectives, gathered_layer(): lax.all_to_all(column_terms.reshape(groups, tokens_dev, -1), 'ep', split_...  20.3 us
    all_gather x1, blocking collectives, gathered_layer(): routed_all = lax.all_gather(routed, 'ep', axis=0, tiled=True)  15.9 us
    sub x1, matrix products, attend_local(): attention_scores - largest  8.38 us
    ppermute x5, starting transfers between devices, swap(): return lax.ppermute(value, 'tp', [(0, 1), (1, 0)])  8.08 us
    dot_general x2, matrix products, down(): lax.dot_general(value, slot, (((1,), (1,)), ((), ())), preferred_element_...  6.21 us
  transfers between devices with their start and end apart: 8, of which 6 were waited for; matrix products, arithmetic and copies ran while one was open for 5% of the time, Pallas kernels for 0%

profile of v5, /device:TPU:0, one launch (start us, length us, event | category | flops | bytes accessed | tf_op | source)
XLA Modules:
  0.0 238.4 jit_solution(14153803762986282373)
XLA Ops:
  6.5 0.0 copy-start
  6.5 0.0 all-gather.3.cloned.1.call-start
  7.3 1.1 copy.47
  8.5 1.3 fusion.38
  9.8 1.3 fusion.37
  11.1 0.2 copy.43
  11.3 1.0 copy.34
  12.3 0.2 copy.30
  12.5 0.1 copy.31
  12.6 0.1 copy.32
  12.8 1.1 fusion.22
  13.8 0.3 concatenate.35
  14.1 8.4 %fusion.39 = (f32[2,8,128]{2,1,0:T(8,128)S(1)}, f32[2,8,128,1152]{2,3,1,0:T(8,128)}) fusion(pred[128,1152]{0,1:T(8,128)(4,1)S(1)} %fusion.22, bf16[128,2,8,128]{3,2,1,0:T(8,128)(2,1)S(1)} %bitcast.91, bf16[64,2,128]{2,0,1:T(8,128)(2,1)S(1)} %get-tuple-element.41, bf16[64,2,128]{2,0,1:T(8,128)(2,1)S(1)} %get-tuple-element.42, bf16[1024,2,128]{2,0,1:T(8,128)(2,1)} %copy.34), kind=kOutput, calls=%fused_computation.73 | convolution fusion | flops 617546880 | bytes 10706944 | tf_op jit(solution)/shard_map/sub | solution.py:45
  22.5 0.0 copy-start.4
  22.5 0.0 copy-start.3
  22.5 0.0 copy-start.5
  22.5 5.4 %fusion.16 = bf16[2,128,8,128]{3,1,2,0:T(8,128)(2,1)} fusion(f32[2,8,128,1152]{2,3,1,0:T(8,128)} %get-tuple-element.36, f32[2,8,128]{2,1,0:T(8,128)S(1)} %get-tuple-element.35, bf16[1152,2,128]{0,2,1:T(8,128)(2,1)S(1)} %concatenate.35), kind=kOutput, calls=%fused_computation.25 | convolution fusion | flops 608960512 | bytes 10559488 | tf_op jit(solution)/shard_map/qizo,oqx->zqix/dot_general | solution.py:47
  27.9 0.0 all-gather.3.cloned.1.call-update
  27.9 0.0 all-gather.5.cloned.1.call-start
  28.0 2.8 %dynamic-slice_bitcast_fusion = bf16[2,1024,384]{2,1,0:T(8,128)(2,1)} fusion(bf16[2,3,1024,384]{3,2,1,0:T(8,128)(2,1)} %param.19, s32[]{:T(128)S(6)} %select_n.74), kind=kLoop, calls=%fused_computation.11 | loop fusion | bytes 3145732 | tf_op jit(solution)/shard_map/slice | solution.py:125
  30.7 3.0 %collective-permute-start = (bf16[2,1024,384]{2,1,0:T(8,128)(2,1)}, bf16[2,1024,384]{2,1,0:T(8,128)(2,1)}, u32[]{:S(2)}, u32[]{:S(2)}) collective-permute-start(bf16[2,1024,384]{2,1,0:T(8,128)(2,1)} %dynamic-slice_bitcast_fusion), channel_id=1, source_target_pairs={{0,1},{1,0},{2,3},{3,2},{4,5},{5,4},{6,7},{7,6},{8,9},{9,8},{10,11... | collective-permute-start | bytes 4718600 | tf_op jit(solution)/shard_map/ppermute | solution.py:99
  33.7 0.0 copy-done.4
  33.7 0.0 collective-permute-start.2
  33.7 0.0 copy-done.3
  33.7 2.0 collective-permute-start.1
  35.7 0.0 copy-done.5
  35.7 0.1 reshape.67
  35.8 15.9 %all_gather.9 = s32[1024,8]{0,1:T(8,128)S(1)} all-gather(s32[128,8]{0,1:T(8,128)S(1)} %reshape.67), channel_id=1, replica_groups=mesh['rep'=2,'ep'=8,'tp'=2] {'ep'}, dimensions={0}, use_global_device_ids=true | all-gather | bytes 36864 | tf_op jit(solution)/shard_map/all_gather | solution.py:136
  51.7 18.2 %collective-permute-done.2 = bf16[1024,16]{0,1:T(8,128)(2,1)S(1)} collective-permute-done((bf16[1024,16]{0,1:T(8,128)(2,1)S(1)}, bf16[1024,16]{0,1:T(8,128)(2,1)S(1)}, u32[]{:S(2)}, u32[]{:S(2)}) %collective-permute-start.2) | collective-permute-done | bytes 32800 | tf_op jit(solution)/shard_map/ppermute | solution.py:99
  69.9 4.7 %collective-permute-done.1 = bf16[128,1024]{1,0:T(8,128)(2,1)S(1)} collective-permute-done((bf16[128,1024]{1,0:T(8,128)(2,1)S(1)}, bf16[128,1024]{1,0:T(8,128)(2,1)S(1)}, u32[]{:S(2)}, u32[]{:S(2)}) %collective-permute-start.1) | collective-permute-done | bytes 262176 | tf_op jit(solution)/shard_map/ppermute | solution.py:99
  74.6 0.1 broadcast_select_fusion.3
  74.7 0.0 collective-permute-done
  74.7 2.2 broadcast_select_fusion.1
  76.9 2.0 pad_maximum_fusion
  78.9 0.0 all-gather.3.cloned.1.call-done
  78.9 0.0 copy-done
  78.9 3.5 %convolution_convert_fusion = bf16[1024,256]{1,0:T(8,128)(2,1)S(1)} fusion(bf16[1024,2048]{0,1:T(8,128)(2,1)} %all-gather.3.cloned.1.call-done, bf16[2048,256]{1,0:T(8,128)(2,1)S(1)} %copy-done), kind=kOutput, calls=%fused_computation.26 | convolution fusion | flops 1074003968 | bytes 5767168 | tf_op jit(solution)/shard_map/dot_general | solution.py:143
  82.4 0.0 copy-start.6
  82.4 20.3 %all_to_all.5 = bf16[8,128,256]{2,1,0:T(8,128)(2,1)S(1)} all-to-all(bf16[8,128,256]{2,1,0:T(8,128)(2,1)S(1)} %bitcast.92), channel_id=1, replica_groups=mesh['rep'=2,'ep'=8,'tp'=2] {'ep'}, dimensions={0} | all-to-all | bytes 1048576 | tf_op jit(solution)/shard_map/all_to_all | solution.py:146
  102.7 1.6 collective-permute-start.3
  104.3 11.8 %collective-permute-done.3 = bf16[128,2048]{1,0:T(8,128)(2,1)S(1)} collective-permute-done((bf16[128,2048]{1,0:T(8,128)(2,1)S(1)}, bf16[128,2048]{1,0:T(8,128)(2,1)S(1)}, u32[]{:S(2)}, u32[]{:S(2)}) %collective-permute-start.3) | collective-permute-done | bytes 524320 | tf_op jit(solution)/shard_map/ppermute | solution.py:99
  116.1 0.4 fusion.18
  116.5 0.9 fusion.19
  117.4 0.0 all-gather.5.cloned.1.call-update
  117.4 0.2 reduce-scatter.2.cloned.1.call-start
  117.7 0.0 copy-done.6
  117.7 0.1 fusion.23
  117.8 46.2 %all-gather.5.cloned.1.call-done = bf16[1024,2048]{1,0:T(8,128)(2,1)} async-done(((bf16[128,2048]{1,0:T(8,128)(2,1)}), bf16[1024,2048]{1,0:T(8,128)(2,1)}) %all-gather.5.cloned.1.call-update) | async-done | bytes 4194320 | tf_op jit(solution)/shard_map/all_gather | solution.py:155
  164.0 0.0 copy-start.1
  164.0 0.0 copy-start.2
  164.0 5.1 %fusion.8 = f32[1024,384]{1,0:T(8,128)S(1)} fusion(bf16[1024,2048]{1,0:T(8,128)(2,1)} %all-gather.5.cloned.1.call-done, bf16[2,2048,384]{2,1,0:T(8,128)(2,1)} %pad_maximum_fusion), kind=kOutput, calls=%fused_computation.15 | convolution fusion | flops 1610612736 | bytes 7340032 | tf_op jit(solution)/shard_map/dot_general | solution.py:164
  169.1 0.0 copy-done.1
  169.1 0.0 copy-done.2
  169.1 2.4 %multiply_convert_fusion = bf16[1024,384]{1,0:T(8,128)(2,1)S(1)} fusion(f32[1024,384]{1,0:T(8,128)S(1)} %fusion.8, bf16[1024,2048]{1,0:T(8,128)(2,1)S(1)} %copy-done.1, bf16[2,2048,384]{2,1,0:T(8,128)(2,1)S(1)} %copy-done.2), kind=kOutput, calls=%fused_computation.17 | convolution fusion | flops 1612972032 | bytes 8126464 | tf_op jit(solution)/shard_map/dot_general | solution.py:165
  171.6 1.5 collective-permute-start.4
  173.1 1.2 fusion.42
  174.3 0.1 select_reduce_fusion.1
  174.4 2.4 %fusion.20 = f32[1024,1024]{1,0:T(8,128)S(1)} fusion(bf16[1024,384]{1,0:T(8,128)(2,1)S(1)} %multiply_convert_fusion, bf16[2,3,1024,384]{3,2,1,0:T(8,128)(2,1)} %param.19, s32[]{:T(128)S(6)} %select_n.73, s32[]{:T(128)S(6)} %add.63), kind=kOutput, calls=%fused_computation.34 | convolution fusion | flops 805306368 | bytes 5767176 | tf_op jit(solution)/shard_map/dot_general | solution.py:158
  176.9 14.5 %collective-permute-done.4 = bf16[1024,384]{1,0:T(8,128)(2,1)S(1)} collective-permute-done((bf16[1024,384]{1,0:T(8,128)(2,1)S(1)}, bf16[1024,384]{1,0:T(8,128)(2,1)S(1)}, u32[]{:S(2)}, u32[]{:S(2)}) %collective-permute-start.4) | collective-permute-done | bytes 786464 | tf_op jit(solution)/shard_map/ppermute | solution.py:99
  191.3 3.8 %add_convert_fusion = bf16[1024,1024]{1,0:T(8,128)(2,1)} fusion(f32[1024,1024]{1,0:T(8,128)S(1)} %fusion.20, bf16[1024,384]{1,0:T(8,128)(2,1)S(1)} %collective-permute-done.4, f32[1024]{0:T(1024)S(1)} %get-tuple-element.18, f32[1024]{0:T(1024)S(1)} %get-tuple-element.17, bf16[2,3,1024,384]{3,2,1,0:T(8,128)(2,1)} %param.19, s32[]{:T(128)S(6)} %select_n.74, ...), kind=kOutput, calls=%fused_computation.9 | convolution fusion | flops 809500672 | bytes 7872520 | tf_op jit(solution)/shard_map/dot_general | solution.py:158
  195.1 0.0 reduce-scatter.2.cloned.1.call-update
  195.1 35.0 %reduce-scatter.2.cloned.1.call-done = bf16[128,1024]{1,0:T(8,128)(2,1)} async-done(((bf16[1024,1024]{1,0:T(8,128)(2,1)}), bf16[128,1024]{1,0:T(8,128)(2,1)}) %reduce-scatter.2.cloned.1.call-update) | async-done | bytes 262160 | tf_op jit(solution)/shard_map/reduce_scatter | solution.py:176
  230.1 1.8 add_convert_fusion.2
  (10 shorter events, 0.2 us)
Async XLA Ops:
  6.5 72.4 %copy-start = (bf16[2048,256]{1,0:T(8,128)(2,1)S(1)}, bf16[2048,256]{1,0:T(8,128)(2,1)}, u32[]{:S(2)}) copy-start(bf16[2048,256]{1,0:T(8,128)(2,1)} %param.17) | copy-start | bytes 3145732
  6.5 72.4 %all-gather.3.cloned.1.call-start = ((), (), s32[]{:S(2)}) async-start(), calls=%async_computation.2 | async-start | bytes 4718592 | tf_op jit(solution)/shard_map/all_gather | solution.py:123
  22.5 11.2 %copy-start.4 = (bf16[1024,16]{0,1:T(8,128)(2,1)S(1)}, bf16[1024,16]{0,1:T(8,128)(2,1)}, u32[]{:S(2)}) copy-start(bf16[1024,16]{0,1:T(8,128)(2,1)} %param.18) | copy-start | bytes 98308
  22.5 11.2 %copy-start.3 = (bf16[2,64,1024]{2,1,0:T(8,128)(2,1)S(1)}, bf16[2,64,1024]{2,1,0:T(8,128)(2,1)}, u32[]{:S(2)}) copy-start(bf16[2,64,1024]{2,1,0:T(8,128)(2,1)} %param.12) | copy-start | bytes 786436
  22.5 13.2 %copy-start.5 = (s32[2,64,8]{1,2,0:T(8,128)S(1)}, s32[2,64,8]{1,2,0:T(8,128)}, u32[]{:S(2)}) copy-start(s32[2,64,8]{1,2,0:T(8,128)} %param.20) | copy-start | bytes 12292
  27.9 136.1 %all-gather.5.cloned.1.call-start = ((), (), s32[]{:S(2)}) async-start(), calls=%async_computation.3 | async-start | bytes 4718592 | tf_op jit(solution)/shard_map/all_gather | solution.py:155
  30.7 44.0 %collective-permute-start = (bf16[2,1024,384]{2,1,0:T(8,128)(2,1)}, bf16[2,1024,384]{2,1,0:T(8,128)(2,1)}, u32[]{:S(2)}, u32[]{:S(2)}) collective-permute-start(bf16[2,1024,384]{2,1,0:T(8,128)(2,1)} %dynamic-slice_bitcast_fusion), channel_id=1, source_target_pairs={{0,1},{1,0},{2,3},{3,2},{4,5},{5,4},{6,7},{7,6},{8,9},{9,8},{10,11... | collective-permute-start | bytes 4718600 | tf_op jit(solution)/shard_map/ppermute | solution.py:99
  33.7 36.2 %collective-permute-start.2 = (bf16[1024,16]{0,1:T(8,128)(2,1)S(1)}, bf16[1024,16]{0,1:T(8,128)(2,1)S(1)}, u32[]{:S(2)}, u32[]{:S(2)}) collective-permute-start(bf16[1024,16]{0,1:T(8,128)(2,1)S(1)} %copy-done.4), channel_id=1, source_target_pairs={{0,1},{1,0},{2,3},{3,2},{4,5},{5,4},{6,7},{7,6},{8,9},{9,8},{10,11... | collective-permute-start | bytes 98312 | tf_op jit(solution)/shard_map/ppermute | solution.py:99
  33.7 40.9 %collective-permute-start.1 = (bf16[128,1024]{1,0:T(8,128)(2,1)S(1)}, bf16[128,1024]{1,0:T(8,128)(2,1)S(1)}, u32[]{:S(2)}, u32[]{:S(2)}) collective-permute-start(bf16[128,1024]{1,0:T(8,128)(2,1)S(1)} %bitcast.95), channel_id=1, source_target_pairs={{0,1},{1,0},{2,3},{3,2},{4,5},{5,4},{6,7},{7,6},{8,9},{9,8},{10,11... | collective-permute-start | bytes 786440 | tf_op jit(solution)/shard_map/ppermute | solution.py:99
  82.4 35.3 %copy-start.6 = (s32[16]{0:T(128)S(1)}, s32[16]{0:T(128)}, u32[]{:S(2)}) copy-start(s32[16]{0:T(128)} %param.21) | copy-start | bytes 196
  102.7 13.4 %collective-permute-start.3 = (bf16[128,2048]{1,0:T(8,128)(2,1)S(1)}, bf16[128,2048]{1,0:T(8,128)(2,1)S(1)}, u32[]{:S(2)}, u32[]{:S(2)}) collective-permute-start(bf16[128,2048]{1,0:T(8,128)(2,1)S(1)} %bitcast.84), channel_id=1, source_target_pairs={{0,1},{1,0},{2,3},{3,2},{4,5},{5,4},{6,7},{7,6},{8,9},{9,8},{10,11... | collective-permute-start | bytes 1572872 | tf_op jit(solution)/shard_map/ppermute | solution.py:99
  117.4 112.7 %reduce-scatter.2.cloned.1.call-start = ((), (), s32[]{:S(2)}) async-start(), calls=%async_computation.4 | async-start | bytes 2359296 | tf_op jit(solution)/shard_map/reduce_scatter | solution.py:176
  164.0 5.1 %copy-start.1 = (bf16[1024,2048]{1,0:T(8,128)(2,1)S(1)}, bf16[1024,2048]{1,0:T(8,128)(2,1)}, u32[]{:S(2)}) copy-start(bf16[1024,2048]{1,0:T(8,128)(2,1)} %all-gather.5.cloned.1.call-done) | copy-start | bytes 12582916
  164.0 5.2 %copy-start.2 = (bf16[2,2048,384]{2,1,0:T(8,128)(2,1)S(1)}, bf16[2,2048,384]{2,1,0:T(8,128)(2,1)}, u32[]{:S(2)}) copy-start(bf16[2,2048,384]{2,1,0:T(8,128)(2,1)} %pad_maximum_fusion) | copy-start | bytes 9437188
  171.6 19.7 %collective-permute-start.4 = (bf16[1024,384]{1,0:T(8,128)(2,1)S(1)}, bf16[1024,384]{1,0:T(8,128)(2,1)S(1)}, u32[]{:S(2)}, u32[]{:S(2)}) collective-permute-start(bf16[1024,384]{1,0:T(8,128)(2,1)S(1)} %multiply_convert_fusion), channel_id=1, source_target_pairs={{0,1},{1,0},{2,3},{3,2},{4,5},{5,4},{6,7},{7,6},{8,9},{9,8},{10,11... | collective-permute-start | bytes 2359304 | tf_op jit(solution)/shard_map/ppermute | solution.py:99
Sparse Core Ops, SparseCore 0:
  28.0 50.6 all-gather.2
  117.6 46.3 all-gather.4
  195.3 34.8 reduce-scatter.1
